TPU v7x, 32 devices: a whole 2x2x4 slice. The times are simulated.
32 devices in a mesh: depth: 4 (over y, core), row: 4 (over z), col: 2 (over x).
Axes of the slice: x: 2, y: 2, z: 4, core: 2. Of those that a mesh axis runs over, the one named last changes fastest.
Arguments:
- left_factor: bfloat16 [1792, 32, 512], P('depth', None, 'row'), may hold values from -6 to 6
- right_factor: bfloat16 [1792, 32, 512], P('depth', None, 'col'), may hold values from -6 to 6
- out_weight: bfloat16 [1024, 128], replicated, may hold values from -12 to 12
- pair_cotangent: bfloat16 [512, 512, 128], P(('row', 'depth'), 'col'), may hold values from -0.29882812 to 0.29882812
Outputs:
- left_grad: float32 [1792, 32, 512], P(('depth', 'col'), None, 'row')
- right_grad: float32 [1792, 32, 512], P(('depth', 'row'), None, 'col')
- weight_grad: float32 [1024, 128], P(('depth', 'row', 'col'))
All inputs are finite; a program needn't handle non-finite values.
Results may differ from a plain program's by a relative error of at most 0.0075.
Values may be sent and summed in bfloat16 or wider, within the bound.
A program may use at most 320 MiB of HBM per device.

v0:
```python
import jax
import jax.numpy as jnp
from jax import lax
from jax.sharding import PartitionSpec as P


def body(left_factor, right_factor, out_weight, pair_cotangent):
    seq_total = left_factor.shape[0] * lax.axis_size("depth")
    chans = left_factor.shape[1]
    rows_here = left_factor.shape[2]
    cols_here = right_factor.shape[2]
    width = out_weight.shape[0]
    pair_ch = out_weight.shape[1]
    natural = (
        jnp.einsum("sci,sej->ciej", left_factor, right_factor, preferred_element_type=jnp.float32)
        / seq_total
    )
    natural = natural.astype(jnp.bfloat16)
    outer = jnp.transpose(natural, (1, 3, 0, 2)).reshape(rows_here, cols_here, width)
    piece = lax.all_gather(pair_cotangent, "depth", axis=0, tiled=True)
    count = piece.shape[0]
    grad_two = piece.reshape(count * cols_here, pair_ch)
    fresh = jnp.dot(grad_two, out_weight.T, preferred_element_type=jnp.float32).astype(jnp.bfloat16)
    delta_acc = fresh.reshape(count, cols_here, width)
    outer_rows = outer.reshape(count * cols_here, width)
    weight_acc = jnp.dot(outer_rows.T, grad_two, preferred_element_type=jnp.float32)
    delta_four = delta_acc.reshape(rows_here, cols_here, chans, chans)
    left_part = (
        jnp.einsum("ijce,sej->sci", delta_four, right_factor, preferred_element_type=jnp.float32)
        / seq_total
    )
    right_part = (
        jnp.einsum("ijce,sci->sej", delta_four, left_factor, preferred_element_type=jnp.float32)
        / seq_total
    )
    left_grad = lax.psum_scatter(left_part, "col", scatter_dimension=0, tiled=True)
    right_grad = lax.psum_scatter(right_part, "row", scatter_dimension=0, tiled=True)
    middle = lax.psum_scatter(weight_acc, ("depth", "row"), scatter_dimension=0, tiled=True)
    weight_grad = lax.psum_scatter(middle, "col", scatter_dimension=0, tiled=True)
    return (left_grad, right_grad, weight_grad)


def solution(mesh):
    return jax.shard_map(
        body,
        mesh=mesh,
        in_specs=(
            P("depth", None, "row"),
            P("depth", None, "col"),
            P(),
            P(("row", "depth"), "col", None),
        ),
        out_specs=(
            P(("depth", "col"), None, "row"),
            P(("depth", "row"), None, "col"),
            P(("depth", "row", "col"), None),
        ),
        check_vma=False,
    )
```

profile of v0, /device:TPU:0, one launch (start us, length us, event | category | flops | bytes accessed | tf_op | source)
XLA Modules:
  0.0 739.4 jit_solution(3225494194948077554)
XLA Ops:
  7.2 0.0 copy-start
  7.2 0.0 all-gather.2.cloned.1.call-start
  7.2 0.7 all-gather.2.cloned.1.call-update
  7.9 0.0 reduce-scatter.9.cloned.1.call-start
  8.0 54.0 %multiply_convert_fusion = bf16[32,128,32,256]{3,1,2,0:T(8,128)(2,1)} fusion(bf16[448,32,256]{2,1,0:T(8,128)(2,1)} %param.5, bf16[448,32,128,1]{2,1,0,3:T(8,128)(2,1)} %bitcast.43), kind=kOutput, calls=%fused_computation | convolution fusion | flops 30131879936 | bytes 78118912 | tf_op jit(solution)/shard_map/sci,sej->ciej/dot_general | solution.py:15
  61.9 59.4 %copy.38 = bf16[128,8,128,256]{3,1,2,0:T(8,128)(2,1)} copy(bf16[128,8,128,256]{3,2,1,0:T(8,128)(2,1)} %bitcast.18) | data formatting | bytes 134217728
  121.3 0.0 all-gather.2.cloned.1.call-done
  121.3 0.0 copy-done
  121.3 29.5 %convolution_convert_fusion = bf16[32768,1024]{1,0:T(8,128)(2,1)} fusion(bf16[32768,128]{1,0:T(8,128)(2,1)} %bitcast.41, bf16[1024,128]{1,0:T(8,128)(2,1)S(1)} %copy-done), kind=kOutput, calls=%fused_computation.1 | convolution fusion | flops 8623489024 | bytes 75759616 | tf_op jit(solution)/shard_map/dot_general | solution.py:23
  150.8 81.3 %copy.23 = bf16[32768,1024]{0,1:T(8,128)(2,1)} copy(bf16[32768,1024]{1,0:T(8,128)(2,1)} %convolution_convert_fusion) | data formatting | bytes 134217728 | tf_op jit(solution)/shard_map/convert_element_type | solution.py:23
  232.1 44.5 %copy.37 = bf16[128,8,128,256]{3,2,1,0:T(8,128)(2,1)} copy(bf16[128,8,128,256]{3,1,2,0:T(8,128)(2,1)} %bitcast.12) | data formatting | bytes 134217728
  276.6 29.9 %fusion.11 = f32[1024,128]{1,0:T(8,128)} fusion(bf16[32768,1024]{0,1:T(8,128)(2,1)} %bitcast.20, bf16[32768,128]{1,0:T(8,128)(2,1)} %bitcast.42), kind=kOutput, calls=%fused_computation.13 | convolution fusion | flops 8589934592 | bytes 76021760 | tf_op jit(solution)/shard_map/dot_general | solution.py:26
  306.5 0.0 reduce-scatter.9.cloned.1.call-update
  306.5 0.0 reduce-scatter.5.cloned.1.call-start
  306.5 73.2 %fusion.1 = f32[448,32,128]{2,0,1:T(8,128)} fusion(bf16[128,256,32,32]{1,0,3,2:T(8,128)(2,1)} %bitcast.15, bf16[448,32,256]{2,1,0:T(8,128)(2,1)} %param.5), kind=kOutput, calls=%fused_computation.5 | convolution fusion | flops 30066606080 | bytes 81788928 | tf_op jit(solution)/shard_map/ijce,sej->sci/dot_general | solution.py:29
  379.7 0.0 reduce-scatter.5.cloned.1.call-update
  379.8 0.0 reduce-scatter.7.cloned.1.call-start
  379.8 39.8 %fusion = f32[448,32,256]{2,0,1:T(8,128)} fusion(bf16[128,256,32,32]{1,0,3,2:T(8,128)(2,1)} %bitcast.15, bf16[448,32,128,1]{2,1,0,3:T(8,128)(2,1)} %bitcast.44), kind=kOutput, calls=%fused_computation.3 | convolution fusion | flops 30068441088 | bytes 85458944 | tf_op jit(solution)/shard_map/ijce,sci->sej/dot_general | solution.py:33
  419.6 0.0 reduce-scatter.7.cloned.1.call-update
  419.6 0.0 reduce-scatter.11.cloned.1.call-start
  419.7 0.0 reduce-scatter.9.cloned.1.call-done
  419.7 0.5 reduce-scatter.11.cloned.1.call-update
  420.2 51.0 %reduce-scatter.5.cloned.1.call-done = f32[224,32,128]{2,0,1:T(8,128)} async-done(((f32[448,32,128]{2,0,1:T(8,128)}), f32[224,32,128]{2,0,1:T(8,128)}) %reduce-scatter.5.cloned.1.call-update) | async-done | bytes 3670032 | tf_op jit(solution)/shard_map/reduce_scatter | solution.py:36
  471.2 6.0 copy.28
  477.2 242.0 %reduce-scatter.7.cloned.1.call-done = f32[112,32,256]{2,0,1:T(8,128)} async-done(((f32[448,32,256]{2,0,1:T(8,128)}), f32[112,32,256]{2,0,1:T(8,128)}) %reduce-scatter.7.cloned.1.call-update) | async-done | bytes 3670032 | tf_op jit(solution)/shard_map/reduce_scatter | solution.py:37
  719.2 6.0 copy.29
  725.2 7.7 %reduce-scatter.11.cloned.1.call-done = f32[32,128]{1,0:T(8,128)} async-done(((f32[64,128]{1,0:T(8,128)}), f32[32,128]{1,0:T(8,128)}) %reduce-scatter.11.cloned.1.call-update) | async-done | bytes 16400 | tf_op jit(solution)/shard_map/reduce_scatter | solution.py:39
Async XLA Ops:
  7.2 114.1 %copy-start = (bf16[1024,128]{1,0:T(8,128)(2,1)S(1)}, bf16[1024,128]{1,0:T(8,128)(2,1)}, u32[]{:S(2)}) copy-start(bf16[1024,128]{1,0:T(8,128)(2,1)} %param.6) | copy-start | bytes 786436
  7.2 114.1 %all-gather.2.cloned.1.call-start = ((), (), s32[]{:S(2)}) async-start(), calls=%async_computation.4 | async-start | bytes 10485760 | tf_op jit(solution)/shard_map/all_gather | solution.py:20
  7.9 411.8 %reduce-scatter.9.cloned.1.call-start = ((), (), s32[]{:S(2)}) async-start(), calls=%async_computation.7 | async-start | bytes 557056 | tf_op jit(solution)/shard_map/reduce_scatter | solution.py:38
  306.5 164.7 %reduce-scatter.5.cloned.1.call-start = ((), (), s32[]{:S(2)}) async-start(), calls=%async_computation.5 | async-start | bytes 11010048 | tf_op jit(solution)/shard_map/reduce_scatter | solution.py:36
  379.8 339.4 %reduce-scatter.7.cloned.1.call-start = ((), (), s32[]{:S(2)}) async-start(), calls=%async_computation.6 | async-start | bytes 18350080 | tf_op jit(solution)/shard_map/reduce_scatter | solution.py:37
  419.6 313.2 %reduce-scatter.11.cloned.1.call-start = ((), (), s32[]{:S(2)}) async-start(), calls=%async_computation.8 | async-start | bytes 49152 | tf_op jit(solution)/shard_map/reduce_scatter | solution.py:39
Sparse Core Ops, SparseCore 0:
  9.5 60.9 all-gather.1
  306.6 58.9 reduce-scatter.8
  379.9 91.3 reduce-scatter.4
  473.4 245.7 reduce-scatter.6
  721.8 11.0 reduce-scatter.10
where the time goes:
time: 742 us; the launch traced here: 739 us
  waiting for transfers between devices  302 us (41%)
  matrix products  226 us (30%)
  local copies, waits for them, and re-layouts  197 us (27%)
  between operations  13.8 us (2%)
    reduce_scatter x1, waiting for transfers between devices, body(): lax.psum_scatter(right_part, 'row', scatter_dimension=0, tiled=True)  242 us
    unnamed x6, local copies, waits for them, and re-layouts  116 us
    convert_element_type x1, local copies, waits for them, and re-layouts, body(): jnp.dot(grad_two, out_weight.T, preferred_element_type=jnp.float32)  81.3 us
    dot_general x1, matrix products, body(): jnp.einsum('ijce,sej->sci', delta_four, right_factor, preferred_element_t...  73.2 us
    dot_general x1, matrix products, body(): jnp.einsum('sci,sej->ciej', left_factor, right_factor, preferred_element_...  54 us
    reduce_scatter x1, waiting for transfers between devices, body(): lax.psum_scatter(left_part, 'col', scatter_dimension=0, tiled=True)  51 us
    dot_general x1, matrix products, body(): jnp.einsum('ijce,sci->sej', delta_four, left_factor, preferred_element_ty...  39.8 us
    dot_general x1, matrix products, body(): jnp.dot(outer_rows.T, grad_two, preferred_element_type=jnp.float32)  29.9 us
  transfers between devices with their start and end apart: 5, of which 3 were waited for; matrix products, arithmetic and copies ran while one was open for 32% of the time, Pallas kernels for 0%

commit v1 on v0

v1 whole, which is shorter than its diff:
```python
import functools

import jax
import jax.numpy as jnp
from jax import lax
from jax.experimental import pallas as pl
from jax.experimental.pallas import tpu as pltpu
from jax.sharding import PartitionSpec as P

F32 = jnp.float32
BF16 = jnp.bfloat16
VMEM_CAP = 60 * 1024 * 1024


def params():
    return pltpu.CompilerParams(vmem_limit_bytes=VMEM_CAP)


def cost(flops, nbytes):
    return pl.CostEstimate(flops=flops, bytes_accessed=nbytes, transcendentals=0)


def outer_kernel(inv, at_ref, b_ref, o_ref):
    width = 512 if o_ref.shape[1] % 512 == 0 else o_ref.shape[1]
    for n in range(o_ref.shape[1] // width):
        cols = slice(n * width, (n + 1) * width)
        acc = jnp.dot(at_ref[...], b_ref[:, cols], preferred_element_type=F32)
        o_ref[:, cols] = (acc * inv).astype(BF16)


def outer_call(at, b2, inv, tm, tn):
    rows, seqs = at.shape
    cols = b2.shape[1]
    return pl.pallas_call(
        functools.partial(outer_kernel, inv),
        out_shape=jax.ShapeDtypeStruct((rows, cols), BF16),
        grid=(cols // tn, rows // tm),
        in_specs=[
            pl.BlockSpec((tm, seqs), lambda n, m: (m, 0)),
            pl.BlockSpec((seqs, tn), lambda n, m: (0, n)),
        ],
        out_specs=pl.BlockSpec((tm, tn), lambda n, m: (m, n)),
        compiler_params=params(),
        cost_estimate=cost(2 * rows * cols * seqs, 2 * rows * cols + 2 * seqs * (rows + cols)),
        name="outer",
    )(at, b2)


def delta_kernel(inv, chans, toks, w_ref, g_ref, a_ref, d_ref, r_ref, acc_ref):
    step = pl.program_id(0)
    here = g_ref.shape[0]
    eb = w_ref.shape[0] // chans

    def one(i, carry):
        d = lax.dot_general(
            w_ref[...], g_ref[i], (((1,), (1,)), ((), ())), preferred_element_type=F32
        ).astype(BF16)
        at = pl.multiple_of(i * chans, chans)
        for e in range(eb):
            d_ref[pl.ds(at, chans), e * toks:(e + 1) * toks] = d[e * chans:(e + 1) * chans]
        return carry

    lax.fori_loop(0, here, one, 0, unroll=8)

    @pl.when(step == 0)
    def _():
        acc_ref[...] = jnp.zeros_like(acc_ref)

    for e in range(eb):
        cols = slice(e * toks, (e + 1) * toks)
        acc_ref[:, cols] += jnp.dot(a_ref[...], d_ref[:, cols], preferred_element_type=F32)

    @pl.when(step == pl.num_programs(0) - 1)
    def _():
        r_ref[...] = (acc_ref[...] * inv).astype(BF16)


def delta_call(w_ec, g, a2, inv, chans, part, eb, ti):
    rows, toks, pair_ch = g.shape
    seqs = a2.shape[0]
    wide = eb * toks
    return pl.pallas_call(
        functools.partial(delta_kernel, inv, chans, toks),
        out_shape=(
            jax.ShapeDtypeStruct((rows * chans, wide), BF16),
            jax.ShapeDtypeStruct((seqs, wide), BF16),
        ),
        grid=(rows // ti,),
        in_specs=[
            pl.BlockSpec((eb * chans, pair_ch), lambda m: (part, 0)),
            pl.BlockSpec((ti, toks, pair_ch), lambda m: (m, 0, 0)),
            pl.BlockSpec((seqs, ti * chans), lambda m: (0, m)),
        ],
        out_specs=(
            pl.BlockSpec((ti * chans, wide), lambda m: (m, 0)),
            pl.BlockSpec((seqs, wide), lambda m: (0, 0)),
        ),
        scratch_shapes=[pltpu.VMEM((seqs, wide), F32)],
        compiler_params=params(),
        cost_estimate=cost(
            2 * rows * chans * wide * (seqs + 2 * pair_ch),
            2 * rows * (chans * wide + toks * pair_ch + chans * seqs),
        ),
        name=f"delta_right_{part}",
    )(w_ec, g, a2)


def left_kernel(inv, parts, b_ref, *refs):
    d_refs, o_ref = refs[:parts], refs[parts]
    wide = d_refs[0].shape[1]
    acc = None
    for k in range(parts):
        term = lax.dot_general(
            b_ref[:, k * wide:(k + 1) * wide],
            d_refs[k][...],
            (((1,), (1,)), ((), ())),
            preferred_element_type=F32,
        )
        acc = term if acc is None else acc + term
    o_ref[...] = acc * inv


def left_call(b2, ds, inv, tn):
    seqs = b2.shape[0]
    rows, wide = ds[0].shape
    parts = len(ds)
    return pl.pallas_call(
        functools.partial(left_kernel, inv, parts),
        out_shape=jax.ShapeDtypeStruct((seqs, rows), F32),
        grid=(rows // tn,),
        in_specs=[pl.BlockSpec((seqs, parts * wide), lambda m: (0, 0))]
        + [pl.BlockSpec((tn, wide), lambda m: (m, 0))] * parts,
        out_specs=pl.BlockSpec((seqs, tn), lambda m: (0, m)),
        compiler_params=params(),
        cost_estimate=cost(2 * seqs * rows * wide * parts, 2 * rows * wide * parts + 4 * seqs * rows),
        name="left",
    )(b2, *ds)


def weight_kernel(chans, o_ref, g_ref, w_ref):
    ti, toks, pair_ch = g_ref.shape
    width = w_ref.shape[0] // chans

    @pl.when(pl.program_id(0) == 0)
    def _():
        w_ref[...] = jnp.zeros_like(w_ref)

    group = 4
    eg = 8 if width % 8 == 0 else 1
    for i0 in range(0, ti, group):
        right = g_ref[i0:i0 + group].reshape(group * toks, pair_ch)
        for e0 in range(0, width, eg):
            left = jnp.concatenate(
                [
                    jnp.concatenate(
                        [
                            o_ref[i * chans:(i + 1) * chans, e * toks:(e + 1) * toks]
                            for i in range(i0, i0 + group)
                        ],
                        axis=1,
                    )
                    for e in range(e0, e0 + eg)
                ],
                axis=0,
            )
            w_ref[e0 * chans:(e0 + eg) * chans] += jnp.dot(left, right, preferred_element_type=F32)


def weight_call(outer, g, chans, ti):
    rows, toks, pair_ch = g.shape
    cols = outer.shape[1]
    width = cols // toks * chans
    return pl.pallas_call(
        functools.partial(weight_kernel, chans),
        out_shape=jax.ShapeDtypeStruct((width, pair_ch), F32),
        grid=(rows // ti,),
        in_specs=[
            pl.BlockSpec((ti * chans, cols), lambda m: (m, 0)),
            pl.BlockSpec((ti, toks, pair_ch), lambda m: (m, 0, 0)),
        ],
        out_specs=pl.BlockSpec((width, pair_ch), lambda m: (0, 0)),
        compiler_params=params(),
        cost_estimate=cost(4 * rows * toks * width * pair_ch, 2 * rows * chans * cols),
        name="weight",
    )(outer, g)


def fused_body(left_factor, right_factor, out_weight, pair_cotangent):
    seqs, chans, rows = left_factor.shape
    toks = right_factor.shape[2]
    pair_ch = out_weight.shape[1]
    inv = 1.0 / (seqs * lax.axis_size("depth"))
    n_col = lax.axis_size("col")
    parts = 4
    eb = chans // parts

    g = lax.all_gather(pair_cotangent, "depth", axis=0, tiled=True)
    a2 = jnp.transpose(left_factor, (0, 2, 1)).reshape(seqs, rows * chans)
    at = jnp.transpose(left_factor, (2, 1, 0)).reshape(rows * chans, seqs)
    b2 = right_factor.reshape(seqs, chans * toks)
    w_ec = jnp.transpose(out_weight.reshape(chans, chans, pair_ch), (1, 0, 2)).reshape(
        chans * chans, pair_ch
    )

    outer = outer_call(at, b2, inv, 16 * chans, eb * toks)
    g, outer = lax.optimization_barrier((g, outer))

    ds, rights = [], []
    for k in range(parts):
        d, r = delta_call(w_ec, g, a2, inv, chans, k, eb, 32)
        ds.append(d)
        rights.append(
            lax.psum_scatter(r.reshape(seqs, eb, toks), "row", scatter_dimension=0, tiled=True)
        )
    left = left_call(b2, ds, inv, 8 * chans)
    left, outer = lax.optimization_barrier((left, outer))
    left = jnp.transpose(left.reshape(seqs, rows, chans), (0, 2, 1))
    if n_col == 2:
        half = seqs // 2
        me = lax.axis_index("col")
        mine = lax.dynamic_slice_in_dim(left, me * half, half, 0)
        theirs = lax.dynamic_slice_in_dim(left, (1 - me) * half, half, 0).astype(BF16)
        got = lax.ppermute(theirs, "col", [(0, 1), (1, 0)])
        left_grad = mine + got.astype(F32)
    else:
        left_grad = lax.psum_scatter(left, "col", scatter_dimension=0, tiled=True)
    weight_acc = weight_call(outer, g, chans, 8)
    weight_acc = jnp.transpose(weight_acc.reshape(chans, chans, pair_ch), (1, 0, 2)).reshape(
        chans * chans, pair_ch
    )
    middle = lax.psum_scatter(weight_acc, ("depth", "row"), scatter_dimension=0, tiled=True)
    weight_grad = lax.psum_scatter(middle, "col", scatter_dimension=0, tiled=True)
    right_grad = jnp.concatenate(rights, axis=1).astype(F32)
    return left_grad, right_grad, weight_grad


def plain_body(left_factor, right_factor, out_weight, pair_cotangent):
    seq_total = left_factor.shape[0] * lax.axis_size("depth")
    chans = left_factor.shape[1]
    rows_here = left_factor.shape[2]
    cols_here = right_factor.shape[2]
    width = out_weight.shape[0]
    pair_ch = out_weight.shape[1]
    natural = jnp.einsum("sci,sej->ciej", left_factor, right_factor, preferred_element_type=F32) / seq_total
    outer = jnp.transpose(natural.astype(BF16), (1, 3, 0, 2)).reshape(rows_here * cols_here, width)
    piece = lax.all_gather(pair_cotangent, "depth", axis=0, tiled=True)
    grad_two = piece.reshape(rows_here * cols_here, pair_ch)
    delta = jnp.dot(grad_two, out_weight.T, preferred_element_type=F32).astype(BF16)
    weight_acc = jnp.dot(outer.T, grad_two, preferred_element_type=F32)
    delta_four = delta.reshape(rows_here, cols_here, chans, chans)
    left_part = jnp.einsum("ijce,sej->sci", delta_four, right_factor, preferred_element_type=F32) / seq_total
    right_part = jnp.einsum("ijce,sci->sej", delta_four, left_factor, preferred_element_type=F32) / seq_total
    left_grad = lax.psum_scatter(left_part, "col", scatter_dimension=0, tiled=True)
    right_grad = lax.psum_scatter(right_part, "row", scatter_dimension=0, tiled=True)
    middle = lax.psum_scatter(weight_acc, ("depth", "row"), scatter_dimension=0, tiled=True)
    weight_grad = lax.psum_scatter(middle, "col", scatter_dimension=0, tiled=True)
    return left_grad, right_grad, weight_grad


def body(left_factor, right_factor, out_weight, pair_cotangent):
    seqs, chans, rows = left_factor.shape
    toks = right_factor.shape[2]
    fits = toks % 128 == 0 and toks <= 256 and rows % 32 == 0 and chans == 32 and seqs <= 512
    run = fused_body if fits else plain_body
    return run(left_factor, right_factor, out_weight, pair_cotangent)


def solution(mesh):
    return jax.shard_map(
        body,
        mesh=mesh,
        in_specs=(
            P("depth", None, "row"),
            P("depth", None, "col"),
            P(),
            P(("row", "depth"), "col", None),
        ),
        out_specs=(
            P(("depth", "col"), None, "row"),
            P(("depth", "row"), None, "col"),
            P(("depth", "row", "col"), None),
        ),
        check_vma=False,
    )
```

time: 742 us -> 498 us (0.67)
  matrix products: 226 us -> 0 us
  Pallas kernels: 0 us -> 205 us
  local copies, waits for them, and re-layouts: 197 us -> 78.1 us
  waiting for transfers between devices: 302 us -> 186 us
  other arithmetic: 0 us -> 9.52 us
    dot_general x5 -> x0, matrix products: 226 us -> none  [the longest x1 73.2 us: body(): jnp.einsum('ijce,sej->sci', delta_four, right_factor, preferred_element_t...]
    pallas_call x0 -> x7, Pallas kernels: none -> 205 us  [the longest x4 81.9 us: delta_call(): pl.pallas_call(functools.partial(delta_kernel, inv, chans, toks), out_sha...]
    reduce_scatter x4 -> x6, waiting for transfers between devices: 301 us -> 173 us  [the longest x4 136 us: fused_body(): lax.psum_scatter(r.reshape(seqs, eb, toks), 'row', scatter_dimension=0, t...]
    unnamed x6 -> x10, local copies, waits for them, and re-layouts: 116 us -> 30.5 us
    convert_element_type x1 -> x2, local copies, waits for them, and re-layouts: 81.3 us -> 6.99 us  [fused_body(): lax.dynamic_slice_in_dim(left, (1 - me) * half, half, 0).astype(BF16)]
    transpose x0 -> x3, local copies, waits for them, and re-layouts: none -> 19.6 us  [the longest x1 8.84 us: fused_body(): a2 = jnp.transpose(left_factor, (0, 2, 1)).reshape(seqs, rows * chans)]
    ppermute x0 -> x1, waiting for transfers between devices: none -> 11.5 us  [fused_body(): got = lax.ppermute(theirs, 'col', [(0, 1), (1, 0)])]
    optimization_barrier x0 -> x1, local copies, waits for them, and re-layouts: none -> 9.08 us  [fused_body(): left, outer = lax.optimization_barrier((left, outer))]
  transfers between devices with their start and end apart: 5 -> 8, of which waited for: 3 -> 7; matrix products, arithmetic and copies ran while one was open for 32% -> 17% of each run, Pallas kernels for 0% -> 10%
where the time goes in v1:
time: 498 us; the launch traced here: 496 us
  Pallas kernels  205 us (41%)
  waiting for transfers between devices  186 us (37%)
  local copies, waits for them, and re-layouts  78.1 us (16%)
  between operations  14.2 us (3%)
  other arithmetic  9.52 us (2%)
    reduce_scatter x4, waiting for transfers between devices, fused_body(): lax.psum_scatter(r.reshape(seqs, eb, toks), 'row', scatter_dimension=0, t...  136 us
    pallas_call x4, Pallas kernels, delta_call(): pl.pallas_call(functools.partial(delta_kernel, inv, chans, toks), out_sha...  81.9 us
    pallas_call x1, Pallas kernels, outer_call(): pl.pallas_call(functools.partial(outer_kernel, inv), out_shape=jax.ShapeD...  50.1 us
    pallas_call x1, Pallas kernels, left_call(): pl.pallas_call(functools.partial(left_kernel, inv, parts), out_shape=jax....  41.4 us
    pallas_call x1, Pallas kernels, weight_call(): pl.pallas_call(functools.partial(weight_kernel, chans), out_shape=jax.Sha...  31.5 us
    unnamed x10, local copies, waits for them, and re-layouts  30.5 us
    reduce_scatter x1, waiting for transfers between devices, fused_body(): lax.psum_scatter(weight_acc, ('depth', 'row'), scatter_dimension=0, tiled...  28.9 us
    ppermute x1, waiting for transfers between devices, fused_body(): got = lax.ppermute(theirs, 'col', [(0, 1), (1, 0)])  11.5 us
  transfers between devices with their start and end apart: 8, of which 7 were waited for; matrix products, arithmetic and copies ran while one was open for 17% of the time, Pallas kernels for 10%

profile of v1, /device:TPU:0, one launch (start us, length us, event | category | flops | bytes accessed | tf_op | source)
XLA Modules:
  0.0 496.0 jit_solution(7094027369005522458)
XLA Ops:
  7.2 0.0 all-gather.2.cloned.1.call-start
  7.2 0.7 all-gather.2.cloned.1.call-update
  7.9 0.0 reduce-scatter.15.cloned.1.call-start
  7.9 1.8 copy.23
  9.7 8.5 %copy.24 = bf16[128,32,448]{2,1,0:T(8,128)(2,1)} copy(bf16[128,32,448]{0,1,2:T(8,128)(2,1)} %bitcast.30) | data formatting | bytes 7340032 | tf_op jit(solution)/shard_map/transpose | solution.py:199
  18.2 8.8 %copy.25 = bf16[448,128,32]{0,2,1:T(8,128)(2,1)} copy(bf16[448,128,32]{1,2,0:T(8,128)(2,1)} %bitcast.31) | data formatting | bytes 7340032 | tf_op jit(solution)/shard_map/transpose | solution.py:198
  27.0 6.3 %copy.26.a_ref = bf16[448,4096]{1,0:T(8,128)(2,1)} copy(bf16[448,4096]{0,1:T(8,128)(2,1)} %bitcast.29) | data formatting | bytes 7340032 | tf_op jit(solution)/shard_map/reshape | solution.py:198
  33.3 14.6 %copy.35 = bf16[56,8,32,256]{3,1,2,0:T(8,128)(2,1)} copy(bf16[56,8,32,256]{3,2,1,0:T(8,128)(2,1)} %bitcast.32) | data formatting | bytes 14680064
  47.9 50.1 %outer.1.o_ref = bf16[4096,8192]{1,0:T(8,128)(2,1)} custom-call(bf16[4096,448]{1,0:T(8,128)(2,1)} %bitcast.39, bf16[448,8192]{1,0:T(8,128)(2,1)} %bitcast.33), custom_call_target="tpu_custom_call" | custom-call | flops 30064771072 | bytes 78118912 | tf_op jit(solution)/shard_map/outer/pallas_call | solution.py:34
  98.1 20.6 %delta_right_3.1 = (bf16[4096,2048]{1,0:T(8,128)(2,1)}, bf16[448,2048]{1,0:T(8,128)(2,1)}) custom-call(bf16[1024,128]{1,0:T(8,128)(2,1)} %bitcast.47, bf16[128,256,128]{2,1,0:T(8,128)(2,1)} %all-gather.2.cloned.1.call-done.g_ref, bf16[448,4096]{1,0:T(8,128)(2,1)} %copy.26.a_ref), custom_call_target="tpu_custom_call" | custom-call | flops 11811160064 | bytes 28835840 | tf_op jit(solution)/shard_map/delta_right_3/pallas_call | solution.py:82
  118.7 20.5 %delta_right_2.1 = (bf16[4096,2048]{1,0:T(8,128)(2,1)}, bf16[448,2048]{1,0:T(8,128)(2,1)}) custom-call(bf16[1024,128]{1,0:T(8,128)(2,1)} %bitcast.48, bf16[128,256,128]{2,1,0:T(8,128)(2,1)} %all-gather.2.cloned.1.call-done.g_ref, bf16[448,4096]{1,0:T(8,128)(2,1)} %copy.26.a_ref), custom_call_target="tpu_custom_call" | custom-call | flops 11811160064 | bytes 28835840 | tf_op jit(solution)/shard_map/delta_right_2/pallas_call | solution.py:82
  139.2 20.4 %delta_right_1.1 = (bf16[4096,2048]{1,0:T(8,128)(2,1)}, bf16[448,2048]{1,0:T(8,128)(2,1)}) custom-call(bf16[1024,128]{1,0:T(8,128)(2,1)} %bitcast.49, bf16[128,256,128]{2,1,0:T(8,128)(2,1)} %all-gather.2.cloned.1.call-done.g_ref, bf16[448,4096]{1,0:T(8,128)(2,1)} %copy.26.a_ref), custom_call_target="tpu_custom_call" | custom-call | flops 11811160064 | bytes 28835840 | tf_op jit(solution)/shard_map/delta_right_1/pallas_call | solution.py:82
  159.6 20.4 %delta_right_0.1 = (bf16[4096,2048]{1,0:T(8,128)(2,1)}, bf16[448,2048]{1,0:T(8,128)(2,1)}) custom-call(bf16[1024,128]{1,0:T(8,128)(2,1)} %bitcast.50, bf16[128,256,128]{2,1,0:T(8,128)(2,1)} %all-gather.2.cloned.1.call-done.g_ref, bf16[448,4096]{1,0:T(8,128)(2,1)} %copy.26.a_ref), custom_call_target="tpu_custom_call" | custom-call | flops 11811160064 | bytes 28835840 | tf_op jit(solution)/shard_map/delta_right_0/pallas_call | solution.py:82
  180.0 41.4 %left.1 = f32[448,4096]{1,0:T(8,128)} custom-call(bf16[448,8192]{1,0:T(8,128)(2,1)} %bitcast.34, bf16[4096,2048]{1,0:T(8,128)(2,1)} %get-tuple-element.16.refs_0_, bf16[4096,2048]{1,0:T(8,128)(2,1)} %get-tuple-element.17.refs_1_, bf16[4096,2048]{1,0:T(8,128)(2,1)} %get-tuple-element.18.refs_2_, bf16[4096,2048]{1,0:T(8,128)(2,1)} %get-tuple-element.19.refs_3_), custom_call_target="tpu_custom_call" | custom-call | flops 30064771072 | bytes 74448896 | tf_op jit(solution)/shard_map/left/pallas_call | solution.py:127
  221.4 31.5 %weight.1 = f32[1024,128]{1,0:T(8,128)} custom-call(bf16[4096,8192]{1,0:T(8,128)(2,1)} %outer.1.o_ref, bf16[128,256,128]{2,1,0:T(8,128)(2,1)} %all-gather.2.cloned.1.call-done.g_ref), custom_call_target="tpu_custom_call" | custom-call | flops 17179869184 | bytes 67108864 | tf_op jit(solution)/shard_map/weight/pallas_call | solution.py:173
  252.9 2.3 copy.33
  255.2 0.0 reduce-scatter.15.cloned.1.call-update
  255.2 0.3 reduce-scatter.13.cloned.1.call-start
  255.5 3.3 copy.39
  258.8 0.0 reduce-scatter.13.cloned.1.call-update
  258.8 0.0 reduce-scatter.11.cloned.1.call-start
  258.9 0.0 copy-done.1
  258.9 1.9 copy.38
  260.8 0.0 reduce-scatter.11.cloned.1.call-update
  260.8 0.0 reduce-scatter.9.cloned.1.call-start
  260.8 3.4 copy.37
  264.3 0.0 reduce-scatter.9.cloned.1.call-update
  264.3 0.0 reduce-scatter.7.cloned.1.call-start
  264.3 0.0 copy-done
  264.4 1.9 copy.36
  266.2 0.0 reduce-scatter.7.cloned.1.call-update
  266.2 0.0 reduce-scatter.17.cloned.1.call-start
  266.3 9.1 %copy.30 = f32[448,4096]{0,1:T(8,128)} copy(f32[448,4096]{1,0:T(8,128)} %left.1) | data formatting | bytes 14680064 | tf_op jit(solution)/shard_map/optimization_barrier | solution.py:216
  275.4 3.6 fusion
  279.0 3.4 copy.31
  282.4 3.0 collective-permute-start
  285.4 28.9 %reduce-scatter.15.cloned.1.call-done = f32[64,128]{1,0:T(8,128)} async-done(((f32[1024,128]{1,0:T(8,128)}), f32[64,128]{1,0:T(8,128)}) %reduce-scatter.15.cloned.1.call-update) | async-done | bytes 32784 | tf_op jit(solution)/shard_map/reduce_scatter | solution.py:231
  314.3 0.0 reduce-scatter.17.cloned.1.call-update
  314.3 11.5 %collective-permute-done = bf16[224,32,128]{2,1,0:T(8,128)(2,1)} collective-permute-done((bf16[224,32,128]{2,1,0:T(8,128)(2,1)}, bf16[224,32,128]{2,1,0:T(8,128)(2,1)}, u32[]{:S(2)}, u32[]{:S(2)}) %collective-permute-start) | collective-permute-done | bytes 1835040 | tf_op jit(solution)/shard_map/ppermute | solution.py:223
  325.8 3.8 copy.32
  329.7 6.0 %bitcast_add_fusion = f32[224,32,128]{0,1,2:T(8,128)} fusion(bf16[224,32,128]{0,1,2:T(8,128)(2,1)S(1)} %copy.32, f32[448,128,32]{0,2,1:T(8,128)} %bitcast.28, s32[]{:T(128)S(6)} %select_n.6), kind=kLoop, calls=%fused_computation | loop fusion | flops 1835008 | bytes 9175044 | tf_op jit(solution)/shard_map/add | solution.py:224
  335.6 5.4 %copy.34 = f32[224,32,128]{2,1,0:T(8,128)} copy(f32[224,32,128]{0,1,2:T(8,128)} %bitcast_add_fusion) | data formatting | bytes 7340032
  341.0 14.1 %reduce-scatter.13.cloned.1.call-done = bf16[112,8,256]{2,1,0:T(8,128)(2,1)} async-done(((bf16[448,8,256]{2,1,0:T(8,128)(2,1)}), bf16[112,8,256]{2,1,0:T(8,128)(2,1)}) %reduce-scatter.13.cloned.1.call-update) | async-done | bytes 458768 | tf_op jit(solution)/shard_map/reduce_scatter | solution.py:213
  355.1 40.7 %reduce-scatter.11.cloned.1.call-done = bf16[112,8,256]{2,1,0:T(8,128)(2,1)} async-done(((bf16[448,8,256]{2,1,0:T(8,128)(2,1)}), bf16[112,8,256]{2,1,0:T(8,128)(2,1)}) %reduce-scatter.11.cloned.1.call-update) | async-done | bytes 458768 | tf_op jit(solution)/shard_map/reduce_scatter | solution.py:213
  395.9 40.7 %reduce-scatter.9.cloned.1.call-done = bf16[112,8,256]{2,1,0:T(8,128)(2,1)} async-done(((bf16[448,8,256]{2,1,0:T(8,128)(2,1)}), bf16[112,8,256]{2,1,0:T(8,128)(2,1)}) %reduce-scatter.9.cloned.1.call-update) | async-done | bytes 458768 | tf_op jit(solution)/shard_map/reduce_scatter | solution.py:213
  436.6 40.7 %reduce-scatter.7.cloned.1.call-done = bf16[112,8,256]{2,1,0:T(8,128)(2,1)} async-done(((bf16[448,8,256]{2,1,0:T(8,128)(2,1)}), bf16[112,8,256]{2,1,0:T(8,128)(2,1)}) %reduce-scatter.7.cloned.1.call-update) | async-done | bytes 458768 | tf_op jit(solution)/shard_map/reduce_scatter | solution.py:213
  477.4 3.6 maximum_convert_fusion
  480.9 8.2 %reduce-scatter.17.cloned.1.call-done = f32[32,128]{1,0:T(8,128)} async-done(((f32[64,128]{1,0:T(8,128)}), f32[32,128]{1,0:T(8,128)}) %reduce-scatter.17.cloned.1.call-update) | async-done | bytes 16400 | tf_op jit(solution)/shard_map/reduce_scatter | solution.py:232
  (3 shorter events, 0.0 us)
Async XLA Ops:
  7.2 90.9 %all-gather.2.cloned.1.call-start = ((), (), s32[]{:S(2)}) async-start(), calls=%async_computation.6 | async-start | bytes 10485760 | tf_op jit(solution)/shard_map/all_gather | solution.py:197
  7.9 306.4 %reduce-scatter.15.cloned.1.call-start = ((), (), s32[]{:S(2)}) async-start(), calls=%async_computation.11 | async-start | bytes 557056 | tf_op jit(solution)/shard_map/reduce_scatter | solution.py:231
  252.9 6.0 %copy-start.1 = (bf16[448,2048]{1,0:T(8,128)(2,1)S(1)}, bf16[448,2048]{1,0:T(8,128)(2,1)}, u32[]{:S(2)}) copy-start(bf16[448,2048]{1,0:T(8,128)(2,1)} %get-tuple-element.24) | copy-start | bytes 5505028
  255.2 99.9 %reduce-scatter.13.cloned.1.call-start = ((), (), s32[]{:S(2)}) async-start(), calls=%async_computation.10 | async-start | bytes 2293760 | tf_op jit(solution)/shard_map/reduce_scatter | solution.py:213
  258.8 137.0 %reduce-scatter.11.cloned.1.call-start = ((), (), s32[]{:S(2)}) async-start(), calls=%async_computation.9 | async-start | bytes 2293760 | tf_op jit(solution)/shard_map/reduce_scatter | solution.py:213
  260.8 3.6 copy-start
  260.8 175.8 %reduce-scatter.9.cloned.1.call-start = ((), (), s32[]{:S(2)}) async-start(), calls=%async_computation.8 | async-start | bytes 2293760 | tf_op jit(solution)/shard_map/reduce_scatter | solution.py:213
  264.3 213.1 %reduce-scatter.7.cloned.1.call-start = ((), (), s32[]{:S(2)}) async-start(), calls=%async_computation.7 | async-start | bytes 2293760 | tf_op jit(solution)/shard_map/reduce_scatter | solution.py:213
  266.2 222.9 %reduce-scatter.17.cloned.1.call-start = ((), (), s32[]{:S(2)}) async-start(), calls=%async_computation.12 | async-start | bytes 49152 | tf_op jit(solution)/shard_map/reduce_scatter | solution.py:232
  282.4 43.4 %collective-permute-start = (bf16[224,32,128]{2,1,0:T(8,128)(2,1)}, bf16[224,32,128]{2,1,0:T(8,128)(2,1)}, u32[]{:S(2)}, u32[]{:S(2)}) collective-permute-start(bf16[224,32,128]{2,1,0:T(8,128)(2,1)} %copy.31), channel_id=1, source_target_pairs={{0,1},{1,0},{2,3},{3,2},{4,5},{5,4},{6,7},{7,6},{8,9},{9,8},{10,11... | collective-permute-start | bytes 5505032 | tf_op jit(solution)/shard_map/ppermute | solution.py:223
Sparse Core Ops, SparseCore 0:
  9.5 60.9 all-gather.1
  255.4 58.8 reduce-scatter.14
  316.6 38.5 reduce-scatter.12
  357.3 38.5 reduce-scatter.10
  398.0 38.5 reduce-scatter.8
  438.8 38.5 reduce-scatter.6
  480.1 8.9 reduce-scatter.16

commit v2 on v1

--- a/solution.py
+++ b/solution.py
@@ -28,21 +28,21 @@
         o_ref[:, cols] = (acc * inv).astype(BF16)
 
 
-def outer_call(at, b2, inv, tm, tn):
+def outer_call(at, b2, inv, tm, tn, part, cols):
     rows, seqs = at.shape
-    cols = b2.shape[1]
+    first = part * cols // tn
     return pl.pallas_call(
         functools.partial(outer_kernel, inv),
         out_shape=jax.ShapeDtypeStruct((rows, cols), BF16),
         grid=(cols // tn, rows // tm),
         in_specs=[
             pl.BlockSpec((tm, seqs), lambda n, m: (m, 0)),
-            pl.BlockSpec((seqs, tn), lambda n, m: (0, n)),
+            pl.BlockSpec((seqs, tn), lambda n, m: (0, n + first)),
         ],
         out_specs=pl.BlockSpec((tm, tn), lambda n, m: (m, n)),
         compiler_params=params(),
         cost_estimate=cost(2 * rows * cols * seqs, 2 * rows * cols + 2 * seqs * (rows + cols)),
-        name="outer",
+        name=f"outer_{part}",
     )(at, b2)
 
 
@@ -117,7 +117,7 @@
             preferred_element_type=F32,
         )
         acc = term if acc is None else acc + term
-    o_ref[...] = acc * inv
+    o_ref[...] = (acc * inv).astype(BF16)
 
 
 def left_call(b2, ds, inv, tn):
@@ -126,7 +126,7 @@
     parts = len(ds)
     return pl.pallas_call(
         functools.partial(left_kernel, inv, parts),
-        out_shape=jax.ShapeDtypeStruct((seqs, rows), F32),
+        out_shape=jax.ShapeDtypeStruct((seqs, rows), BF16),
         grid=(rows // tn,),
         in_specs=[pl.BlockSpec((seqs, parts * wide), lambda m: (0, 0))]
         + [pl.BlockSpec((tn, wide), lambda m: (m, 0))] * parts,
@@ -137,52 +137,53 @@
     )(b2, *ds)
 
 
-def weight_kernel(chans, o_ref, g_ref, w_ref):
+def weight_kernel(chans, *refs):
+    o_refs, g_ref, w_ref = refs[:-2], refs[-2], refs[-1]
     ti, toks, pair_ch = g_ref.shape
-    width = w_ref.shape[0] // chans
+    per = o_refs[0].shape[1] // toks
 
     @pl.when(pl.program_id(0) == 0)
     def _():
         w_ref[...] = jnp.zeros_like(w_ref)
 
     group = 4
-    eg = 8 if width % 8 == 0 else 1
+    eg = 8 if per % 8 == 0 else 1
     for i0 in range(0, ti, group):
         right = g_ref[i0:i0 + group].reshape(group * toks, pair_ch)
-        for e0 in range(0, width, eg):
-            left = jnp.concatenate(
-                [
-                    jnp.concatenate(
-                        [
-                            o_ref[i * chans:(i + 1) * chans, e * toks:(e + 1) * toks]
-                            for i in range(i0, i0 + group)
-                        ],
-                        axis=1,
-                    )
-                    for e in range(e0, e0 + eg)
-                ],
-                axis=0,
-            )
-            w_ref[e0 * chans:(e0 + eg) * chans] += jnp.dot(left, right, preferred_element_type=F32)
-
-
-def weight_call(outer, g, chans, ti):
+        for h, o_ref in enumerate(o_refs):
+            for e0 in range(0, per, eg):
+                left = jnp.concatenate(
+                    [
+                        jnp.concatenate(
+                            [
+                                o_ref[i * chans:(i + 1) * chans, e * toks:(e + 1) * toks]
+                                for i in range(i0, i0 + group)
+                            ],
+                            axis=1,
+                        )
+                        for e in range(e0, e0 + eg)
+                    ],
+                    axis=0,
+                )
+                at = (h * per + e0) * chans
+                w_ref[at:at + eg * chans] += jnp.dot(left, right, preferred_element_type=F32)
+
+
+def weight_call(outers, g, chans, ti):
     rows, toks, pair_ch = g.shape
-    cols = outer.shape[1]
-    width = cols // toks * chans
+    cols = outers[0].shape[1]
+    width = cols * len(outers) // toks * chans
     return pl.pallas_call(
         functools.partial(weight_kernel, chans),
         out_shape=jax.ShapeDtypeStruct((width, pair_ch), F32),
         grid=(rows // ti,),
-        in_specs=[
-            pl.BlockSpec((ti * chans, cols), lambda m: (m, 0)),
-            pl.BlockSpec((ti, toks, pair_ch), lambda m: (m, 0, 0)),
-        ],
+        in_specs=[pl.BlockSpec((ti * chans, cols), lambda m: (m, 0))] * len(outers)
+        + [pl.BlockSpec((ti, toks, pair_ch), lambda m: (m, 0, 0))],
         out_specs=pl.BlockSpec((width, pair_ch), lambda m: (0, 0)),
         compiler_params=params(),
-        cost_estimate=cost(4 * rows * toks * width * pair_ch, 2 * rows * chans * cols),
+        cost_estimate=cost(4 * rows * toks * width * pair_ch, 2 * rows * toks * width),
         name="weight",
-    )(outer, g)
+    )(*outers, g)
 
 
 def fused_body(left_factor, right_factor, out_weight, pair_cotangent):
@@ -202,32 +203,35 @@
         chans * chans, pair_ch
     )
 
-    outer = outer_call(at, b2, inv, 16 * chans, eb * toks)
-    g, outer = lax.optimization_barrier((g, outer))
+    half_cols = b2.shape[1] // 2
+    outer_a = outer_call(at, b2, inv, 16 * chans, eb * toks, 0, half_cols)
+    g, outer_a = lax.optimization_barrier((g, outer_a))
 
     ds, rights = [], []
     for k in range(parts):
         d, r = delta_call(w_ec, g, a2, inv, chans, k, eb, 32)
         ds.append(d)
-        rights.append(
-            lax.psum_scatter(r.reshape(seqs, eb, toks), "row", scatter_dimension=0, tiled=True)
-        )
+        r, g = lax.optimization_barrier((r.reshape(seqs, eb, toks), g))
+        rights.append(lax.psum_scatter(r, "row", scatter_dimension=0, tiled=True))
     left = left_call(b2, ds, inv, 8 * chans)
-    left, outer = lax.optimization_barrier((left, outer))
     left = jnp.transpose(left.reshape(seqs, rows, chans), (0, 2, 1))
+    left, at, b2 = lax.optimization_barrier((left, at, b2))
     if n_col == 2:
         half = seqs // 2
         me = lax.axis_index("col")
         mine = lax.dynamic_slice_in_dim(left, me * half, half, 0)
-        theirs = lax.dynamic_slice_in_dim(left, (1 - me) * half, half, 0).astype(BF16)
+        theirs = lax.dynamic_slice_in_dim(left, (1 - me) * half, half, 0)
+        theirs, at, b2 = lax.optimization_barrier((theirs, at, b2))
         got = lax.ppermute(theirs, "col", [(0, 1), (1, 0)])
-        left_grad = mine + got.astype(F32)
+        left_grad = mine.astype(F32) + got.astype(F32)
     else:
-        left_grad = lax.psum_scatter(left, "col", scatter_dimension=0, tiled=True)
-    weight_acc = weight_call(outer, g, chans, 8)
+        left_grad = lax.psum_scatter(left, "col", scatter_dimension=0, tiled=True).astype(F32)
+    outer_b = outer_call(at, b2, inv, 16 * chans, eb * toks, 1, half_cols)
+    weight_acc = weight_call((outer_a, outer_b), g, chans, 4)
     weight_acc = jnp.transpose(weight_acc.reshape(chans, chans, pair_ch), (1, 0, 2)).reshape(
         chans * chans, pair_ch
     )
+    weight_acc, *rights = lax.optimization_barrier((weight_acc, *rights))
     middle = lax.psum_scatter(weight_acc, ("depth", "row"), scatter_dimension=0, tiled=True)
     weight_grad = lax.psum_scatter(middle, "col", scatter_dimension=0, tiled=True)
     right_grad = jnp.concatenate(rights, axis=1).astype(F32)

time: 498 us -> 373 us (0.75)
  waiting for transfers between devices: 186 us -> 52.7 us
  Pallas kernels: 205 us -> 215 us
    reduce_scatter x4, waiting for transfers between devices: 136 us -> 0.02 us  [fused_body(): rights.append(lax.psum_scatter(r, 'row', scatter_dimension=0, tiled=True))]
    reduce_scatter x1, waiting for transfers between devices: 28.9 us -> 42.3 us  [fused_body(): lax.psum_scatter(weight_acc, ('depth', 'row'), scatter_dimension=0, tiled...]
    ppermute x1, waiting for transfers between devices: 11.5 us -> 0.01 us  [fused_body(): got = lax.ppermute(theirs, 'col', [(0, 1), (1, 0)])]
    pallas_call x1, Pallas kernels: 31.5 us -> 40.3 us  [weight_call(): pl.pallas_call(functools.partial(weight_kernel, chans), out_shape=jax.Sha...]
    convert_element_type x2 -> x0, local copies, waits for them, and re-layouts: 6.99 us -> none  [fused_body(): lax.dynamic_slice_in_dim(left, (1 - me) * half, half, 0).astype(BF16)]
    pallas_call x0 -> x1, local copies, waits for them, and re-layouts: none -> 6.43 us  [left_call(): pl.pallas_call(functools.partial(left_kernel, inv, parts), out_shape=jax....]
    optimization_barrier x1, local copies, waits for them, and re-layouts: 9.08 us -> 3.38 us  [fused_body(): theirs, at, b2 = lax.optimization_barrier((theirs, at, b2))]
    unnamed x10 -> x14, local copies, waits for them, and re-layouts: 30.5 us -> 33.6 us
  transfers between devices with their start and end apart: 8 -> 8, of which waited for: 7 -> 2; matrix products, arithmetic and copies ran while one was open for 17% -> 22% of each run, Pallas kernels for 10% -> 53%
where the time goes in v2:
time: 373 us; the launch traced here: 370 us
  Pallas kernels  215 us (58%)
  local copies, waits for them, and re-layouts  77.7 us (21%)
  waiting for transfers between devices  52.7 us (14%)
  between operations  14.2 us (4%)
  other arithmetic  7 us (2%)
    pallas_call x4, Pallas kernels, delta_call(): pl.pallas_call(functools.partial(delta_kernel, inv, chans, toks), out_sha...  82 us
    pallas_call x2, Pallas kernels, outer_call(): pl.pallas_call(functools.partial(outer_kernel, inv), out_shape=jax.ShapeD...  51.7 us
    reduce_scatter x1, waiting for transfers between devices, fused_body(): lax.psum_scatter(weight_acc, ('depth', 'row'), scatter_dimension=0, tiled...  42.3 us
    pallas_call x1, Pallas kernels, left_call(): pl.pallas_call(functools.partial(left_kernel, inv, parts), out_shape=jax....  41 us
    pallas_call x1, Pallas kernels, weight_call(): pl.pallas_call(functools.partial(weight_kernel, chans), out_shape=jax.Sha...  40.3 us
    unnamed x14, local copies, waits for them, and re-layouts  33.6 us
    reduce_scatter x1, waiting for transfers between devices, fused_body(): lax.psum_scatter(middle, 'col', scatter_dimension=0, tiled=True)  9.57 us
    transpose x1, local copies, waits for them, and re-layouts, fused_body(): a2 = jnp.transpose(left_factor, (0, 2, 1)).reshape(seqs, rows * chans)  8.83 us
  transfers between devices with their start and end apart: 8, of which 2 were waited for; matrix products, arithmetic and copies ran while one was open for 22% of the time, Pallas kernels for 53%

profile of v2, /device:TPU:0, one launch (start us, length us, event | category | flops | bytes accessed | tf_op | source)
XLA Modules:
  0.0 370.3 jit_solution(7947800937598909726)
XLA Ops:
  7.2 0.0 all-gather.2.cloned.1.call-start
  7.2 0.7 all-gather.2.cloned.1.call-update
  7.9 0.0 reduce-scatter.7.cloned.1.call-start
  7.9 1.8 copy.22
  9.7 8.5 %copy.23 = bf16[128,32,448]{2,1,0:T(8,128)(2,1)} copy(bf16[128,32,448]{0,1,2:T(8,128)(2,1)} %bitcast.28) | data formatting | bytes 7340032 | tf_op jit(solution)/shard_map/transpose | solution.py:200
  18.2 8.8 %copy.24 = bf16[448,128,32]{0,2,1:T(8,128)(2,1)} copy(bf16[448,128,32]{1,2,0:T(8,128)(2,1)} %bitcast.29) | data formatting | bytes 7340032 | tf_op jit(solution)/shard_map/transpose | solution.py:199
  27.0 6.3 %copy.25.a_ref = bf16[448,4096]{1,0:T(8,128)(2,1)} copy(bf16[448,4096]{0,1:T(8,128)(2,1)} %bitcast.27) | data formatting | bytes 7340032 | tf_op jit(solution)/shard_map/reshape | solution.py:199
  33.3 14.6 %copy.34 = bf16[56,8,32,256]{3,1,2,0:T(8,128)(2,1)} copy(bf16[56,8,32,256]{3,2,1,0:T(8,128)(2,1)} %bitcast.30) | data formatting | bytes 14680064
  47.9 25.7 %outer_0.1.refs_0_ = bf16[4096,4096]{1,0:T(8,128)(2,1)} custom-call(bf16[4096,448]{1,0:T(8,128)(2,1)} %bitcast.38, bf16[448,8192]{1,0:T(8,128)(2,1)} %bitcast.31), custom_call_target="tpu_custom_call" | custom-call | flops 15032385536 | bytes 40894464 | tf_op jit(solution)/shard_map/outer_0/pallas_call | solution.py:34
  73.6 20.6 %delta_right_0.1 = (bf16[4096,2048]{1,0:T(8,128)(2,1)}, bf16[448,2048]{1,0:T(8,128)(2,1)}) custom-call(bf16[1024,128]{1,0:T(8,128)(2,1)} %bitcast.47, bf16[128,256,128]{2,1,0:T(8,128)(2,1)} %all-gather.2.cloned.1.call-done.g_ref.refs_2_, bf16[448,4096]{1,0:T(8,128)(2,1)} %copy.25.a_ref), custom_call_target="tpu_custom_call" | custom-call | flops 11811160064 | bytes 28835840 | tf_op jit(solution)/shard_map/delta_right_0/pallas_call | solution.py:82
  94.2 3.4 copy.35
  97.6 0.0 reduce-scatter.7.cloned.1.call-update
  97.6 0.0 reduce-scatter.9.cloned.1.call-start
  97.6 20.4 %delta_right_1.1 = (bf16[4096,2048]{1,0:T(8,128)(2,1)}, bf16[448,2048]{1,0:T(8,128)(2,1)}) custom-call(bf16[1024,128]{1,0:T(8,128)(2,1)} %bitcast.48, bf16[128,256,128]{2,1,0:T(8,128)(2,1)} %all-gather.2.cloned.1.call-done.g_ref.refs_2_, bf16[448,4096]{1,0:T(8,128)(2,1)} %copy.25.a_ref), custom_call_target="tpu_custom_call" | custom-call | flops 11811160064 | bytes 28835840 | tf_op jit(solution)/shard_map/delta_right_1/pallas_call | solution.py:82
  118.1 3.4 copy.36
  121.4 0.0 reduce-scatter.9.cloned.1.call-update
  121.5 0.0 reduce-scatter.11.cloned.1.call-start
  121.5 20.5 %delta_right_2.1 = (bf16[4096,2048]{1,0:T(8,128)(2,1)}, bf16[448,2048]{1,0:T(8,128)(2,1)}) custom-call(bf16[1024,128]{1,0:T(8,128)(2,1)} %bitcast.49, bf16[128,256,128]{2,1,0:T(8,128)(2,1)} %all-gather.2.cloned.1.call-done.g_ref.refs_2_, bf16[448,4096]{1,0:T(8,128)(2,1)} %copy.25.a_ref), custom_call_target="tpu_custom_call" | custom-call | flops 11811160064 | bytes 28835840 | tf_op jit(solution)/shard_map/delta_right_2/pallas_call | solution.py:82
  142.0 3.4 copy.37
  145.3 0.0 reduce-scatter.11.cloned.1.call-update
  145.4 0.0 reduce-scatter.13.cloned.1.call-start
  145.4 20.5 %delta_right_3.1 = (bf16[4096,2048]{1,0:T(8,128)(2,1)}, bf16[448,2048]{1,0:T(8,128)(2,1)}) custom-call(bf16[1024,128]{1,0:T(8,128)(2,1)} %bitcast.50, bf16[128,256,128]{2,1,0:T(8,128)(2,1)} %all-gather.2.cloned.1.call-done.g_ref.refs_2_, bf16[448,4096]{1,0:T(8,128)(2,1)} %copy.25.a_ref), custom_call_target="tpu_custom_call" | custom-call | flops 11811160064 | bytes 28835840 | tf_op jit(solution)/shard_map/delta_right_3/pallas_call | solution.py:82
  165.9 3.4 copy.38
  169.3 0.0 reduce-scatter.13.cloned.1.call-update
  169.3 0.0 reduce-scatter.15.cloned.1.call-start
  169.4 41.0 %left.1 = bf16[448,4096]{1,0:T(8,128)(2,1)} custom-call(bf16[448,8192]{1,0:T(8,128)(2,1)} %bitcast.32, bf16[4096,2048]{1,0:T(8,128)(2,1)} %get-tuple-element.33.refs_0_, bf16[4096,2048]{1,0:T(8,128)(2,1)} %get-tuple-element.36.refs_1_, bf16[4096,2048]{1,0:T(8,128)(2,1)} %get-tuple-element.39.refs_2_, bf16[4096,2048]{1,0:T(8,128)(2,1)} %get-tuple-element.42.refs_3_), custom_call_target="tpu_custom_call" | custom-call | flops 30064771072 | bytes 74448896 | tf_op jit(solution)/shard_map/left/pallas_call | solution.py:127
  210.4 6.4 %copy.29 = bf16[448,4096]{0,1:T(8,128)(2,1)} copy(bf16[448,4096]{1,0:T(8,128)(2,1)} %left.1) | data formatting | bytes 7340032 | tf_op jit(solution)/shard_map/left/pallas_call | solution.py:127
  216.8 3.0 constant_dynamic-slice_fusion
  219.8 3.4 copy.30
  223.2 3.4 collective-permute-start
  226.6 25.9 %outer_1.1.refs_1_ = bf16[4096,4096]{1,0:T(8,128)(2,1)} custom-call(bf16[4096,448]{1,0:T(8,128)(2,1)} %bitcast.39, bf16[448,8192]{1,0:T(8,128)(2,1)} %bitcast.33), custom_call_target="tpu_custom_call" | custom-call | flops 15032385536 | bytes 40894464 | tf_op jit(solution)/shard_map/outer_1/pallas_call | solution.py:34
  252.5 40.3 %weight.1 = f32[1024,128]{1,0:T(8,128)} custom-call(bf16[4096,4096]{1,0:T(8,128)(2,1)} %outer_0.1.refs_0_, bf16[4096,4096]{1,0:T(8,128)(2,1)} %outer_1.1.refs_1_, bf16[128,256,128]{2,1,0:T(8,128)(2,1)} %all-gather.2.cloned.1.call-done.g_ref.refs_2_), custom_call_target="tpu_custom_call" | custom-call | flops 17179869184 | bytes 67108864 | tf_op jit(solution)/shard_map/weight/pallas_call | solution.py:176
  292.8 2.1 copy.32
  294.9 0.0 reduce-scatter.13.cloned.1.call-done
  295.0 0.0 reduce-scatter.15.cloned.1.call-update
  295.0 0.0 reduce-scatter.17.cloned.1.call-start
  295.0 0.0 collective-permute-done
  295.0 3.8 %copy.31 = bf16[224,32,128]{0,1,2:T(8,128)(2,1)S(1)} copy(bf16[224,32,128]{2,1,0:T(8,128)(2,1)} %collective-permute-done) | data formatting | bytes 3670016 | tf_op jit(solution)/shard_map/ppermute | solution.py:225
  298.9 4.9 %convert_add_fusion = f32[224,32,128]{0,1,2:T(8,128)} fusion(bf16[224,32,128]{0,1,2:T(8,128)(2,1)S(1)} %copy.31, bf16[448,32,128]{0,1,2:T(8,128)(2,1)} %bitcast.26, s32[]{:T(128)S(6)} %select_n.6), kind=kLoop, calls=%fused_computation | loop fusion | flops 2752512 | bytes 7340036 | tf_op jit(solution)/shard_map/add | solution.py:226
  303.8 5.6 %copy.33 = f32[224,32,128]{2,1,0:T(8,128)} copy(f32[224,32,128]{0,1,2:T(8,128)} %convert_add_fusion) | data formatting | bytes 7340032
  309.3 42.3 %reduce-scatter.15.cloned.1.call-done = f32[64,128]{1,0:T(8,128)} async-done(((f32[1024,128]{1,0:T(8,128)}), f32[64,128]{1,0:T(8,128)}) %reduce-scatter.15.cloned.1.call-update) | async-done | bytes 32784 | tf_op jit(solution)/shard_map/reduce_scatter | solution.py:235
  351.6 0.0 reduce-scatter.17.cloned.1.call-update
  351.7 0.0 copy-done
  351.7 0.0 copy-done.1
  351.7 0.0 copy-done.2
  351.7 0.0 copy-done.3
  351.7 2.1 maximum_convert_fusion
  353.8 9.6 %reduce-scatter.17.cloned.1.call-done = f32[32,128]{1,0:T(8,128)} async-done(((f32[64,128]{1,0:T(8,128)}), f32[32,128]{1,0:T(8,128)}) %reduce-scatter.17.cloned.1.call-update) | async-done | bytes 16400 | tf_op jit(solution)/shard_map/reduce_scatter | solution.py:236
  (8 shorter events, 0.0 us)
Async XLA Ops:
  7.2 66.4 %all-gather.2.cloned.1.call-start = ((), (), s32[]{:S(2)}) async-start(), calls=%async_computation.6 | async-start | bytes 10485760 | tf_op jit(solution)/shard_map/all_gather | solution.py:198
  7.9 287.0 %reduce-scatter.7.cloned.1.call-start = ((), (), s32[]{:S(2)}) async-start(), calls=%async_computation.7 | async-start | bytes 2293760 | tf_op jit(solution)/shard_map/reduce_scatter | solution.py:215
  97.6 197.4 %reduce-scatter.9.cloned.1.call-start = ((), (), s32[]{:S(2)}) async-start(), calls=%async_computation.8 | async-start | bytes 2293760 | tf_op jit(solution)/shard_map/reduce_scatter | solution.py:215
  121.5 173.5 %reduce-scatter.11.cloned.1.call-start = ((), (), s32[]{:S(2)}) async-start(), calls=%async_computation.9 | async-start | bytes 2293760 | tf_op jit(solution)/shard_map/reduce_scatter | solution.py:215
  145.4 149.6 %reduce-scatter.13.cloned.1.call-start = ((), (), s32[]{:S(2)}) async-start(), calls=%async_computation.10 | async-start | bytes 2293760 | tf_op jit(solution)/shard_map/reduce_scatter | solution.py:215
  169.3 182.3 %reduce-scatter.15.cloned.1.call-start = ((), (), s32[]{:S(2)}) async-start(), calls=%async_computation.11 | async-start | bytes 557056 | tf_op jit(solution)/shard_map/reduce_scatter | solution.py:235
  223.2 71.8 %collective-permute-start = (bf16[224,32,128]{2,1,0:T(8,128)(2,1)}, bf16[224,32,128]{2,1,0:T(8,128)(2,1)}, u32[]{:S(2)}, u32[]{:S(2)}) collective-permute-start(bf16[224,32,128]{2,1,0:T(8,128)(2,1)} %copy.30), channel_id=1, source_target_pairs={{0,1},{1,0},{2,3},{3,2},{4,5},{5,4},{6,7},{7,6},{8,9},{9,8},{10,11... | collective-permute-start | bytes 5505032 | tf_op jit(solution)/shard_map/ppermute | solution.py:225
  295.0 68.4 %reduce-scatter.17.cloned.1.call-start = ((), (), s32[]{:S(2)}) async-start(), calls=%async_computation.12 | async-start | bytes 49152 | tf_op jit(solution)/shard_map/reduce_scatter | solution.py:236
  303.8 47.9 %copy-start = (bf16[112,8,256]{2,1,0:T(8,128)(2,1)S(1)}, bf16[112,8,256]{2,1,0:T(8,128)(2,1)}, u32[]{:S(2)}) copy-start(bf16[112,8,256]{2,1,0:T(8,128)(2,1)} %reduce-scatter.7.cloned.1.call-done) | copy-start | bytes 1376260
  303.8 47.9 %copy-start.1 = (bf16[112,8,256]{2,1,0:T(8,128)(2,1)S(1)}, bf16[112,8,256]{2,1,0:T(8,128)(2,1)}, u32[]{:S(2)}) copy-start(bf16[112,8,256]{2,1,0:T(8,128)(2,1)} %reduce-scatter.9.cloned.1.call-done) | copy-start | bytes 1376260
  303.8 47.9 %copy-start.2 = (bf16[112,8,256]{2,1,0:T(8,128)(2,1)S(1)}, bf16[112,8,256]{2,1,0:T(8,128)(2,1)}, u32[]{:S(2)}) copy-start(bf16[112,8,256]{2,1,0:T(8,128)(2,1)} %reduce-scatter.11.cloned.1.call-done) | copy-start | bytes 1376260
  303.8 47.9 %copy-start.3 = (bf16[112,8,256]{2,1,0:T(8,128)(2,1)S(1)}, bf16[112,8,256]{2,1,0:T(8,128)(2,1)}, u32[]{:S(2)}) copy-start(bf16[112,8,256]{2,1,0:T(8,128)(2,1)} %reduce-scatter.13.cloned.1.call-done) | copy-start | bytes 1376260
Sparse Core Ops, SparseCore 0:
  9.5 60.9 all-gather.1
  97.7 42.1 reduce-scatter.6
  142.2 38.5 reduce-scatter.8
  182.9 38.5 reduce-scatter.10
  223.7 38.5 reduce-scatter.12
  295.1 56.4 reduce-scatter.14
  354.4 8.9 reduce-scatter.16

commit v3 on v2

--- a/solution.py
+++ b/solution.py
@@ -148,16 +148,21 @@
 
     group = 4
     eg = 8 if per % 8 == 0 else 1
-    for i0 in range(0, ti, group):
-        right = g_ref[i0:i0 + group].reshape(group * toks, pair_ch)
+
+    def one(k, carry):
+        first = pl.multiple_of(k * group, group)
+        right = g_ref[pl.ds(first, group)].reshape(group * toks, pair_ch)
         for h, o_ref in enumerate(o_refs):
             for e0 in range(0, per, eg):
                 left = jnp.concatenate(
                     [
                         jnp.concatenate(
                             [
-                                o_ref[i * chans:(i + 1) * chans, e * toks:(e + 1) * toks]
-                                for i in range(i0, i0 + group)
+                                o_ref[
+                                    pl.ds(pl.multiple_of((first + i) * chans, chans), chans),
+                                    e * toks:(e + 1) * toks,
+                                ]
+                                for i in range(group)
                             ],
                             axis=1,
                         )
@@ -167,6 +172,9 @@
                 )
                 at = (h * per + e0) * chans
                 w_ref[at:at + eg * chans] += jnp.dot(left, right, preferred_element_type=F32)
+        return carry
+
+    lax.fori_loop(0, ti // group, one, 0)
 
 
 def weight_call(outers, g, chans, ti):
@@ -211,10 +219,9 @@
     for k in range(parts):
         d, r = delta_call(w_ec, g, a2, inv, chans, k, eb, 32)
         ds.append(d)
-        r, g = lax.optimization_barrier((r.reshape(seqs, eb, toks), g))
+        r, g = lax.optimization_barrier((r, g))
         rights.append(lax.psum_scatter(r, "row", scatter_dimension=0, tiled=True))
     left = left_call(b2, ds, inv, 8 * chans)
-    left = jnp.transpose(left.reshape(seqs, rows, chans), (0, 2, 1))
     left, at, b2 = lax.optimization_barrier((left, at, b2))
     if n_col == 2:
         half = seqs // 2
@@ -226,14 +233,18 @@
         left_grad = mine.astype(F32) + got.astype(F32)
     else:
         left_grad = lax.psum_scatter(left, "col", scatter_dimension=0, tiled=True).astype(F32)
+    left_grad = jnp.transpose(left_grad.reshape(-1, rows, chans), (0, 2, 1))
     outer_b = outer_call(at, b2, inv, 16 * chans, eb * toks, 1, half_cols)
-    weight_acc = weight_call((outer_a, outer_b), g, chans, 4)
+    weight_acc = weight_call((outer_a, outer_b), g, chans, 8)
     weight_acc = jnp.transpose(weight_acc.reshape(chans, chans, pair_ch), (1, 0, 2)).reshape(
         chans * chans, pair_ch
     )
-    weight_acc, *rights = lax.optimization_barrier((weight_acc, *rights))
-    middle = lax.psum_scatter(weight_acc, ("depth", "row"), scatter_dimension=0, tiled=True)
-    weight_grad = lax.psum_scatter(middle, "col", scatter_dimension=0, tiled=True)
+    axes = ("depth", "row", "col")
+    count = lax.axis_size(axes)
+    pieces = weight_acc.reshape(count, chans * chans // count, pair_ch)
+    pieces = lax.all_to_all(pieces, axes, split_axis=0, concat_axis=0, tiled=True)
+    weight_grad = jnp.sum(pieces, axis=0)
+    rights = [r.reshape(-1, eb, toks) for r in rights]
     right_grad = jnp.concatenate(rights, axis=1).astype(F32)
     return left_grad, right_grad, weight_grad
 

time: 373 us -> 316 us (0.85)
  waiting for transfers between devices: 52.7 us -> 17.1 us
  local copies, waits for them, and re-layouts: 77.7 us -> 59 us
  Pallas kernels: 215 us -> 208 us
  starting transfers between devices: 3.64 us -> 8.03 us
    reduce_scatter x2 -> x0, waiting for transfers between devices: 51.9 us -> none  [the longest x1 42.3 us: fused_body(): lax.psum_scatter(weight_acc, ('depth', 'row'), scatter_dimension=0, tiled...]
    all_to_all x0 -> x1, waiting for transfers between devices: none -> 16.2 us  [fused_body(): lax.all_to_all(pieces, axes, split_axis=0, concat_axis=0, tiled=True)]
    unnamed x14 -> x6, local copies, waits for them, and re-layouts: 33.6 us -> 24.5 us
    pallas_call x1, Pallas kernels: 40.3 us -> 33 us  [weight_call(): pl.pallas_call(functools.partial(weight_kernel, chans), out_shape=jax.Sha...]
    pallas_call x1 -> x0, local copies, waits for them, and re-layouts: 6.43 us -> none  [left_call(): pl.pallas_call(functools.partial(left_kernel, inv, parts), out_shape=jax....]
    add x0 -> x1, local copies, waits for them, and re-layouts: none -> 5.36 us  [fused_body(): left_grad = mine.astype(F32) + got.astype(F32)]
    all_to_all x0 -> x1, starting transfers between devices: none -> 4.81 us  [fused_body(): lax.all_to_all(pieces, axes, split_axis=0, concat_axis=0, tiled=True)]
    ppermute x1 -> x0, local copies, waits for them, and re-layouts: 3.83 us -> none  [fused_body(): got = lax.ppermute(theirs, 'col', [(0, 1), (1, 0)])]
  transfers between devices with their start and end apart: 8 -> 7, of which waited for: 2 -> 1; matrix products, arithmetic and copies ran while one was open for 22% -> 20% of each run, Pallas kernels for 53% -> 60%
where the time goes in v3:
time: 316 us; the launch traced here: 313 us
  Pallas kernels  208 us (66%)
  local copies, waits for them, and re-layouts  59 us (19%)
  waiting for transfers between devices  17.1 us (5%)
  between operations  13.9 us (4%)
  starting transfers between devices  8.03 us (3%)
  other arithmetic  7.27 us (2%)
    pallas_call x4, Pallas kernels, delta_call(): pl.pallas_call(functools.partial(delta_kernel, inv, chans, toks), out_sha...  82.2 us
    pallas_call x2, Pallas kernels, outer_call(): pl.pallas_call(functools.partial(outer_kernel, inv), out_shape=jax.ShapeD...  52 us
    pallas_call x1, Pallas kernels, left_call(): pl.pallas_call(functools.partial(left_kernel, inv, parts), out_shape=jax....  41 us
    pallas_call x1, Pallas kernels, weight_call(): pl.pallas_call(functools.partial(weight_kernel, chans), out_shape=jax.Sha...  33 us
    unnamed x6, local copies, waits for them, and re-layouts  24.5 us
    all_to_all x1, waiting for transfers between devices, fused_body(): lax.all_to_all(pieces, axes, split_axis=0, concat_axis=0, tiled=True)  16.2 us
    transpose x1, local copies, waits for them, and re-layouts, fused_body(): a2 = jnp.transpose(left_factor, (0, 2, 1)).reshape(seqs, rows * chans)  8.82 us
    transpose x1, local copies, waits for them, and re-layouts, fused_body(): at = jnp.transpose(left_factor, (2, 1, 0)).reshape(rows * chans, seqs)  8.5 us
  transfers between devices with their start and end apart: 7, of which 1 were waited for; matrix products, arithmetic and copies ran while one was open for 20% of the time, Pallas kernels for 60%

profile of v3, /device:TPU:0, one launch (start us, length us, event | category | flops | bytes accessed | tf_op | source)
XLA Modules:
  0.0 313.4 jit_solution(10853593931918606125)
XLA Ops:
  7.2 0.0 all-gather.2.cloned.1.call-start
  7.2 0.7 all-gather.2.cloned.1.call-update
  7.9 0.0 reduce-scatter.5.cloned.1.call-start
  7.9 1.8 copy.20
  9.7 8.5 %copy.21 = bf16[128,32,448]{2,1,0:T(8,128)(2,1)} copy(bf16[128,32,448]{0,1,2:T(8,128)(2,1)} %bitcast.27) | data formatting | bytes 7340032 | tf_op jit(solution)/shard_map/transpose | solution.py:208
  18.2 8.8 %copy.22 = bf16[448,128,32]{0,2,1:T(8,128)(2,1)} copy(bf16[448,128,32]{1,2,0:T(8,128)(2,1)} %bitcast.28) | data formatting | bytes 7340032 | tf_op jit(solution)/shard_map/transpose | solution.py:207
  27.0 6.3 %copy.23.a_ref = bf16[448,4096]{1,0:T(8,128)(2,1)} copy(bf16[448,4096]{0,1:T(8,128)(2,1)} %bitcast.26) | data formatting | bytes 7340032 | tf_op jit(solution)/shard_map/reshape | solution.py:207
  33.3 14.6 %copy.30 = bf16[56,8,32,256]{3,1,2,0:T(8,128)(2,1)} copy(bf16[56,8,32,256]{3,2,1,0:T(8,128)(2,1)} %bitcast.29) | data formatting | bytes 14680064
  47.9 25.9 %outer_0.1.refs_0_ = bf16[4096,4096]{1,0:T(8,128)(2,1)} custom-call(bf16[4096,448]{1,0:T(8,128)(2,1)} %bitcast.33, bf16[448,8192]{1,0:T(8,128)(2,1)} %bitcast.30), custom_call_target="tpu_custom_call" | custom-call | flops 15032385536 | bytes 40894464 | tf_op jit(solution)/shard_map/outer_0/pallas_call | solution.py:34
  73.9 0.0 all-gather.2.cloned.1.call-done.g_ref.refs_2_
  73.9 20.6 %delta_right_0.1 = (bf16[4096,2048]{1,0:T(8,128)(2,1)}, bf16[448,2048]{1,0:T(8,128)(2,1)}) custom-call(bf16[1024,128]{1,0:T(8,128)(2,1)} %bitcast.45, bf16[128,256,128]{2,1,0:T(8,128)(2,1)} %all-gather.2.cloned.1.call-done.g_ref.refs_2_, bf16[448,4096]{1,0:T(8,128)(2,1)} %copy.23.a_ref), custom_call_target="tpu_custom_call" | custom-call | flops 11811160064 | bytes 28835840 | tf_op jit(solution)/shard_map/delta_right_0/pallas_call | solution.py:82
  94.4 0.0 reduce-scatter.5.cloned.1.call-update
  94.5 0.0 reduce-scatter.7.cloned.1.call-start
  94.5 20.4 %delta_right_1.1 = (bf16[4096,2048]{1,0:T(8,128)(2,1)}, bf16[448,2048]{1,0:T(8,128)(2,1)}) custom-call(bf16[1024,128]{1,0:T(8,128)(2,1)} %bitcast.46, bf16[128,256,128]{2,1,0:T(8,128)(2,1)} %all-gather.2.cloned.1.call-done.g_ref.refs_2_, bf16[448,4096]{1,0:T(8,128)(2,1)} %copy.23.a_ref), custom_call_target="tpu_custom_call" | custom-call | flops 11811160064 | bytes 28835840 | tf_op jit(solution)/shard_map/delta_right_1/pallas_call | solution.py:82
  114.9 0.0 reduce-scatter.7.cloned.1.call-update
  114.9 0.0 reduce-scatter.9.cloned.1.call-start
  115.0 20.5 %delta_right_2.1 = (bf16[4096,2048]{1,0:T(8,128)(2,1)}, bf16[448,2048]{1,0:T(8,128)(2,1)}) custom-call(bf16[1024,128]{1,0:T(8,128)(2,1)} %bitcast.47, bf16[128,256,128]{2,1,0:T(8,128)(2,1)} %all-gather.2.cloned.1.call-done.g_ref.refs_2_, bf16[448,4096]{1,0:T(8,128)(2,1)} %copy.23.a_ref), custom_call_target="tpu_custom_call" | custom-call | flops 11811160064 | bytes 28835840 | tf_op jit(solution)/shard_map/delta_right_2/pallas_call | solution.py:82
  135.5 0.0 reduce-scatter.9.cloned.1.call-update
  135.5 0.0 reduce-scatter.11.cloned.1.call-start
  135.5 20.7 %delta_right_3.1 = (bf16[4096,2048]{1,0:T(8,128)(2,1)}, bf16[448,2048]{1,0:T(8,128)(2,1)}) custom-call(bf16[1024,128]{1,0:T(8,128)(2,1)} %bitcast.48, bf16[128,256,128]{2,1,0:T(8,128)(2,1)} %all-gather.2.cloned.1.call-done.g_ref.refs_2_, bf16[448,4096]{1,0:T(8,128)(2,1)} %copy.23.a_ref), custom_call_target="tpu_custom_call" | custom-call | flops 11811160064 | bytes 28835840 | tf_op jit(solution)/shard_map/delta_right_3/pallas_call | solution.py:82
  156.3 41.0 %left.1 = bf16[448,4096]{1,0:T(8,128)(2,1)} custom-call(bf16[448,8192]{1,0:T(8,128)(2,1)} %bitcast.31, bf16[4096,2048]{1,0:T(8,128)(2,1)} %get-tuple-element.28.refs_0_, bf16[4096,2048]{1,0:T(8,128)(2,1)} %get-tuple-element.31.refs_1_, bf16[4096,2048]{1,0:T(8,128)(2,1)} %get-tuple-element.34.refs_2_, bf16[4096,2048]{1,0:T(8,128)(2,1)} %get-tuple-element.37.refs_3_), custom_call_target="tpu_custom_call" | custom-call | flops 30064771072 | bytes 74448896 | tf_op jit(solution)/shard_map/left/pallas_call | solution.py:127
  197.3 1.6 constant_dynamic-slice_fusion
  198.9 3.0 collective-permute-start
  201.9 0.0 reduce-scatter.11.cloned.1.call-update
  201.9 26.1 %outer_1.1.refs_1_ = bf16[4096,4096]{1,0:T(8,128)(2,1)} custom-call(bf16[4096,448]{1,0:T(8,128)(2,1)} %bitcast.34, bf16[448,8192]{1,0:T(8,128)(2,1)} %bitcast.32), custom_call_target="tpu_custom_call" | custom-call | flops 15032385536 | bytes 40894464 | tf_op jit(solution)/shard_map/outer_1/pallas_call | solution.py:34
  228.0 33.0 %weight.1 = f32[1024,128]{1,0:T(8,128)} custom-call(bf16[4096,4096]{1,0:T(8,128)(2,1)} %outer_0.1.refs_0_, bf16[4096,4096]{1,0:T(8,128)(2,1)} %outer_1.1.refs_1_, bf16[128,256,128]{2,1,0:T(8,128)(2,1)} %all-gather.2.cloned.1.call-done.g_ref.refs_2_), custom_call_target="tpu_custom_call" | custom-call | flops 17179869184 | bytes 67108864 | tf_op jit(solution)/shard_map/weight/pallas_call | solution.py:184
  261.0 2.2 copy.36
  263.2 4.8 %all-to-all-start = ((f32[32,32,128]{2,1,0:T(8,128)}), f32[32,32,128]{2,1,0:T(8,128)S(1)}, u32[]{:S(2)}, u32[]{:S(2)}) async-start(f32[32,32,128]{2,1,0:T(8,128)} %bitcast.24), calls=%async_computation.4 | async-start | bytes 1048576 | tf_op jit(solution)/shard_map/all_to_all | solution.py:245
  268.0 16.2 %all-to-all-done = f32[32,32,128]{2,1,0:T(8,128)S(1)} async-done(((f32[32,32,128]{2,1,0:T(8,128)}), f32[32,32,128]{2,1,0:T(8,128)S(1)}, u32[]{:S(2)}, u32[]{:S(2)}) %all-to-all-start) | async-done | bytes 524320 | tf_op jit(solution)/shard_map/all_to_all | solution.py:245
  284.2 0.6 reduce_sum.9
  284.9 0.0 collective-permute-done
  284.9 4.5 %convert_add_fusion = f32[224,4096]{1,0:T(8,128)} fusion(bf16[224,4096]{1,0:T(8,128)(2,1)} %collective-permute-done, bf16[448,4096]{1,0:T(8,128)(2,1)} %left.1, s32[]{:T(128)S(6)} %select_n.6), kind=kLoop, calls=%fused_computation | loop fusion | flops 2752512 | bytes 7340036 | tf_op jit(solution)/shard_map/add | solution.py:233
  289.4 5.4 %copy.27 = f32[224,4096]{0,1:T(8,128)} copy(f32[224,4096]{1,0:T(8,128)} %convert_add_fusion) | data formatting | bytes 7340032 | tf_op jit(solution)/shard_map/add | solution.py:233
  294.7 5.4 %copy.29 = f32[224,32,128]{2,1,0:T(8,128)} copy(f32[224,32,128]{0,1,2:T(8,128)} %bitcast.25) | data formatting | bytes 7340032
  300.1 0.0 reduce-scatter.5.cloned.1.call-done
  300.1 1.1 copy.31
  301.3 0.0 reduce-scatter.7.cloned.1.call-done
  301.3 1.1 copy.32
  302.4 0.0 reduce-scatter.9.cloned.1.call-done
  302.4 1.1 copy.33
  303.6 0.0 reduce-scatter.11.cloned.1.call-done
  303.6 1.1 copy.34
  304.7 2.1 maximum_convert_fusion
Async XLA Ops:
  7.2 66.7 %all-gather.2.cloned.1.call-start = ((), (), s32[]{:S(2)}) async-start(), calls=%async_computation.5 | async-start | bytes 10485760 | tf_op jit(solution)/shard_map/all_gather | solution.py:206
  7.9 292.2 %reduce-scatter.5.cloned.1.call-start = ((), (), s32[]{:S(2)}) async-start(), calls=%async_computation.6 | async-start | bytes 2293760 | tf_op jit(solution)/shard_map/reduce_scatter | solution.py:223
  94.5 206.8 %reduce-scatter.7.cloned.1.call-start = ((), (), s32[]{:S(2)}) async-start(), calls=%async_computation.7 | async-start | bytes 2293760 | tf_op jit(solution)/shard_map/reduce_scatter | solution.py:223
  114.9 187.5 %reduce-scatter.9.cloned.1.call-start = ((), (), s32[]{:S(2)}) async-start(), calls=%async_computation.8 | async-start | bytes 2293760 | tf_op jit(solution)/shard_map/reduce_scatter | solution.py:223
  135.5 168.1 %reduce-scatter.11.cloned.1.call-start = ((), (), s32[]{:S(2)}) async-start(), calls=%async_computation.9 | async-start | bytes 2293760 | tf_op jit(solution)/shard_map/reduce_scatter | solution.py:223
  198.9 86.0 %collective-permute-start = (bf16[224,4096]{1,0:T(8,128)(2,1)S(1)}, bf16[224,4096]{1,0:T(8,128)(2,1)}, u32[]{:S(2)}, u32[]{:S(2)}) collective-permute-start(bf16[224,4096]{1,0:T(8,128)(2,1)S(1)} %constant_dynamic-slice_fusion), channel_id=1, source_target_pairs={{0,1},{1,0},{2,3},{3,2},{4,5},{5,4},{6,7},{7,6},{8,9},{9,8},{10,11... | collective-permute-start | bytes 5505032 | tf_op jit(solution)/shard_map/ppermute | solution.py:232
  263.2 21.0 %all-to-all-start = ((f32[32,32,128]{2,1,0:T(8,128)}), f32[32,32,128]{2,1,0:T(8,128)S(1)}, u32[]{:S(2)}, u32[]{:S(2)}) async-start(f32[32,32,128]{2,1,0:T(8,128)} %bitcast.24), calls=%async_computation.4 | async-start | bytes 1048576 | tf_op jit(solution)/shard_map/all_to_all | solution.py:245
Sparse Core Ops, SparseCore 0:
  9.5 60.9 all-gather.1
  94.6 42.2 reduce-scatter.4
  139.2 38.5 reduce-scatter.6
  180.0 38.5 reduce-scatter.8
  220.7 38.5 reduce-scatter.10

commit v4 on v3

--- a/solution.py
+++ b/solution.py
@@ -243,9 +243,10 @@
     count = lax.axis_size(axes)
     pieces = weight_acc.reshape(count, chans * chans // count, pair_ch)
     pieces = lax.all_to_all(pieces, axes, split_axis=0, concat_axis=0, tiled=True)
-    weight_grad = jnp.sum(pieces, axis=0)
     rights = [r.reshape(-1, eb, toks) for r in rights]
     right_grad = jnp.concatenate(rights, axis=1).astype(F32)
+    pieces, left_grad, right_grad = lax.optimization_barrier((pieces, left_grad, right_grad))
+    weight_grad = jnp.sum(pieces, axis=0)
     return left_grad, right_grad, weight_grad
 
 

time: 316 us -> 299 us (0.946)
  waiting for transfers between devices: 17.1 us -> 0.82 us
    all_to_all x1, waiting for transfers between devices: 16.2 us -> 0.01 us  [fused_body(): lax.all_to_all(pieces, axes, split_axis=0, concat_axis=0, tiled=True)]
  transfers between devices with their start and end apart: 7 -> 7, of which waited for: 1 -> 0; matrix products, arithmetic and copies ran while one was open for 20% -> 20% of each run, Pallas kernels for 60% -> 63%
where the time goes in v4:
time: 299 us; the launch traced here: 297 us
  Pallas kernels  208 us (70%)
  local copies, waits for them, and re-layouts  59 us (20%)
  between operations  13.9 us (5%)
  starting transfers between devices  8.03 us (3%)
  other arithmetic  7.28 us (2%)
    pallas_call x4, Pallas kernels, delta_call(): pl.pallas_call(functools.partial(delta_kernel, inv, chans, toks), out_sha...  82.2 us
    pallas_call x2, Pallas kernels, outer_call(): pl.pallas_call(functools.partial(outer_kernel, inv), out_shape=jax.ShapeD...  52 us
    pallas_call x1, Pallas kernels, left_call(): pl.pallas_call(functools.partial(left_kernel, inv, parts), out_shape=jax....  41 us
    pallas_call x1, Pallas kernels, weight_call(): pl.pallas_call(functools.partial(weight_kernel, chans), out_shape=jax.Sha...  33 us
    unnamed x6, local copies, waits for them, and re-layouts  24.5 us
    transpose x1, local copies, waits for them, and re-layouts, fused_body(): a2 = jnp.transpose(left_factor, (0, 2, 1)).reshape(seqs, rows * chans)  8.82 us
    transpose x1, local copies, waits for them, and re-layouts, fused_body(): at = jnp.transpose(left_factor, (2, 1, 0)).reshape(rows * chans, seqs)  8.5 us
    reshape x1, local copies, waits for them, and re-layouts, fused_body(): a2 = jnp.transpose(left_factor, (0, 2, 1)).reshape(seqs, rows * chans)  6.26 us
  transfers between devices with their start and end apart: 7, of which 0 were waited for; matrix products, arithmetic and copies ran while one was open for 20% of the time, Pallas kernels for 63%

profile of v4, /device:TPU:0, one launch (start us, length us, event | category | flops | bytes accessed | tf_op | source)
XLA Modules:
  0.0 297.2 jit_solution(5467914708011548505)
XLA Ops:
  7.2 0.0 all-gather.2.cloned.1.call-start
  7.2 0.7 all-gather.2.cloned.1.call-update
  7.9 0.0 reduce-scatter.5.cloned.1.call-start
  7.9 1.8 copy.21
  9.7 8.5 %copy.20 = bf16[128,32,448]{2,1,0:T(8,128)(2,1)} copy(bf16[128,32,448]{0,1,2:T(8,128)(2,1)} %bitcast.27) | data formatting | bytes 7340032 | tf_op jit(solution)/shard_map/transpose | solution.py:208
  18.2 8.8 %copy.22 = bf16[448,128,32]{0,2,1:T(8,128)(2,1)} copy(bf16[448,128,32]{1,2,0:T(8,128)(2,1)} %bitcast.28) | data formatting | bytes 7340032 | tf_op jit(solution)/shard_map/transpose | solution.py:207
  27.0 6.3 %copy.23.a_ref = bf16[448,4096]{1,0:T(8,128)(2,1)} copy(bf16[448,4096]{0,1:T(8,128)(2,1)} %bitcast.26) | data formatting | bytes 7340032 | tf_op jit(solution)/shard_map/reshape | solution.py:207
  33.3 14.6 %copy.30 = bf16[56,8,32,256]{3,1,2,0:T(8,128)(2,1)} copy(bf16[56,8,32,256]{3,2,1,0:T(8,128)(2,1)} %bitcast.29) | data formatting | bytes 14680064
  47.9 25.9 %outer_0.1.refs_0_ = bf16[4096,4096]{1,0:T(8,128)(2,1)} custom-call(bf16[4096,448]{1,0:T(8,128)(2,1)} %bitcast.33, bf16[448,8192]{1,0:T(8,128)(2,1)} %bitcast.30), custom_call_target="tpu_custom_call" | custom-call | flops 15032385536 | bytes 40894464 | tf_op jit(solution)/shard_map/outer_0/pallas_call | solution.py:34
  73.9 0.0 all-gather.2.cloned.1.call-done.g_ref.refs_2_
  73.9 20.6 %delta_right_0.1 = (bf16[4096,2048]{1,0:T(8,128)(2,1)}, bf16[448,2048]{1,0:T(8,128)(2,1)}) custom-call(bf16[1024,128]{1,0:T(8,128)(2,1)} %bitcast.45, bf16[128,256,128]{2,1,0:T(8,128)(2,1)} %all-gather.2.cloned.1.call-done.g_ref.refs_2_, bf16[448,4096]{1,0:T(8,128)(2,1)} %copy.23.a_ref), custom_call_target="tpu_custom_call" | custom-call | flops 11811160064 | bytes 28835840 | tf_op jit(solution)/shard_map/delta_right_0/pallas_call | solution.py:82
  94.4 0.0 reduce-scatter.5.cloned.1.call-update
  94.5 0.0 reduce-scatter.7.cloned.1.call-start
  94.5 20.4 %delta_right_1.1 = (bf16[4096,2048]{1,0:T(8,128)(2,1)}, bf16[448,2048]{1,0:T(8,128)(2,1)}) custom-call(bf16[1024,128]{1,0:T(8,128)(2,1)} %bitcast.46, bf16[128,256,128]{2,1,0:T(8,128)(2,1)} %all-gather.2.cloned.1.call-done.g_ref.refs_2_, bf16[448,4096]{1,0:T(8,128)(2,1)} %copy.23.a_ref), custom_call_target="tpu_custom_call" | custom-call | flops 11811160064 | bytes 28835840 | tf_op jit(solution)/shard_map/delta_right_1/pallas_call | solution.py:82
  114.9 0.0 reduce-scatter.7.cloned.1.call-update
  114.9 0.0 reduce-scatter.9.cloned.1.call-start
  115.0 20.5 %delta_right_2.1 = (bf16[4096,2048]{1,0:T(8,128)(2,1)}, bf16[448,2048]{1,0:T(8,128)(2,1)}) custom-call(bf16[1024,128]{1,0:T(8,128)(2,1)} %bitcast.47, bf16[128,256,128]{2,1,0:T(8,128)(2,1)} %all-gather.2.cloned.1.call-done.g_ref.refs_2_, bf16[448,4096]{1,0:T(8,128)(2,1)} %copy.23.a_ref), custom_call_target="tpu_custom_call" | custom-call | flops 11811160064 | bytes 28835840 | tf_op jit(solution)/shard_map/delta_right_2/pallas_call | solution.py:82
  135.5 0.0 reduce-scatter.9.cloned.1.call-update
  135.5 0.0 reduce-scatter.11.cloned.1.call-start
  135.5 20.7 %delta_right_3.1 = (bf16[4096,2048]{1,0:T(8,128)(2,1)}, bf16[448,2048]{1,0:T(8,128)(2,1)}) custom-call(bf16[1024,128]{1,0:T(8,128)(2,1)} %bitcast.48, bf16[128,256,128]{2,1,0:T(8,128)(2,1)} %all-gather.2.cloned.1.call-done.g_ref.refs_2_, bf16[448,4096]{1,0:T(8,128)(2,1)} %copy.23.a_ref), custom_call_target="tpu_custom_call" | custom-call | flops 11811160064 | bytes 28835840 | tf_op jit(solution)/shard_map/delta_right_3/pallas_call | solution.py:82
  156.3 41.0 %left.1 = bf16[448,4096]{1,0:T(8,128)(2,1)} custom-call(bf16[448,8192]{1,0:T(8,128)(2,1)} %bitcast.31, bf16[4096,2048]{1,0:T(8,128)(2,1)} %get-tuple-element.32.refs_0_, bf16[4096,2048]{1,0:T(8,128)(2,1)} %get-tuple-element.35.refs_1_, bf16[4096,2048]{1,0:T(8,128)(2,1)} %get-tuple-element.38.refs_2_, bf16[4096,2048]{1,0:T(8,128)(2,1)} %get-tuple-element.41.refs_3_), custom_call_target="tpu_custom_call" | custom-call | flops 30064771072 | bytes 74448896 | tf_op jit(solution)/shard_map/left/pallas_call | solution.py:127
  197.3 1.6 constant_dynamic-slice_fusion
  198.9 3.0 %collective-permute-start = (bf16[224,4096]{1,0:T(8,128)(2,1)S(1)}, bf16[224,4096]{1,0:T(8,128)(2,1)}, u32[]{:S(2)}, u32[]{:S(2)}) collective-permute-start(bf16[224,4096]{1,0:T(8,128)(2,1)S(1)} %constant_dynamic-slice_fusion), channel_id=1, source_target_pairs={{0,1},{1,0},{2,3},{3,2},{4,5},{5,4},{6,7},{7,6},{8,9},{9,8},{10,11... | collective-permute-start | bytes 5505032 | tf_op jit(solution)/shard_map/ppermute | solution.py:232
  201.9 0.0 reduce-scatter.11.cloned.1.call-update
  201.9 26.1 %outer_1.1.refs_1_ = bf16[4096,4096]{1,0:T(8,128)(2,1)} custom-call(bf16[4096,448]{1,0:T(8,128)(2,1)} %bitcast.34, bf16[448,8192]{1,0:T(8,128)(2,1)} %bitcast.32), custom_call_target="tpu_custom_call" | custom-call | flops 15032385536 | bytes 40894464 | tf_op jit(solution)/shard_map/outer_1/pallas_call | solution.py:34
  228.0 33.0 %weight.1 = f32[1024,128]{1,0:T(8,128)} custom-call(bf16[4096,4096]{1,0:T(8,128)(2,1)} %outer_0.1.refs_0_, bf16[4096,4096]{1,0:T(8,128)(2,1)} %outer_1.1.refs_1_, bf16[128,256,128]{2,1,0:T(8,128)(2,1)} %all-gather.2.cloned.1.call-done.g_ref.refs_2_), custom_call_target="tpu_custom_call" | custom-call | flops 17179869184 | bytes 67108864 | tf_op jit(solution)/shard_map/weight/pallas_call | solution.py:184
  261.0 2.2 copy.36
  263.2 4.8 %all-to-all-start = ((f32[32,32,128]{2,1,0:T(8,128)}), f32[32,32,128]{2,1,0:T(8,128)S(1)}, u32[]{:S(2)}, u32[]{:S(2)}) async-start(f32[32,32,128]{2,1,0:T(8,128)} %bitcast.24), calls=%async_computation | async-start | bytes 1048576 | tf_op jit(solution)/shard_map/all_to_all | solution.py:245
  268.0 0.0 collective-permute-done
  268.0 4.5 %convert_add_fusion = f32[224,4096]{1,0:T(8,128)} fusion(bf16[224,4096]{1,0:T(8,128)(2,1)} %collective-permute-done, bf16[448,4096]{1,0:T(8,128)(2,1)} %left.1, s32[]{:T(128)S(6)} %select_n.7), kind=kLoop, calls=%fused_computation | loop fusion | flops 2752512 | bytes 7340036 | tf_op jit(solution)/shard_map/add | solution.py:233
  272.5 5.4 %copy.28 = f32[224,4096]{0,1:T(8,128)} copy(f32[224,4096]{1,0:T(8,128)} %convert_add_fusion) | data formatting | bytes 7340032 | tf_op jit(solution)/shard_map/add | solution.py:233
  277.9 0.0 reduce-scatter.5.cloned.1.call-done
  277.9 1.1 copy.31
  279.0 0.0 reduce-scatter.7.cloned.1.call-done
  279.0 1.1 copy.32
  280.1 0.0 reduce-scatter.9.cloned.1.call-done
  280.2 1.1 copy.33
  281.3 0.0 reduce-scatter.11.cloned.1.call-done
  281.3 1.1 copy.34
  282.4 2.1 maximum_convert_fusion
  284.6 0.0 all-to-all-done
  284.6 5.4 %copy.29 = f32[224,32,128]{2,1,0:T(8,128)} copy(f32[224,32,128]{0,1,2:T(8,128)} %bitcast.25) | data formatting | bytes 7340032
  290.0 0.6 reduce_sum.9
Async XLA Ops:
  7.2 66.7 %all-gather.2.cloned.1.call-start = ((), (), s32[]{:S(2)}) async-start(), calls=%async_computation.5 | async-start | bytes 10485760 | tf_op jit(solution)/shard_map/all_gather | solution.py:206
  7.9 270.0 %reduce-scatter.5.cloned.1.call-start = ((), (), s32[]{:S(2)}) async-start(), calls=%async_computation.6 | async-start | bytes 2293760 | tf_op jit(solution)/shard_map/reduce_scatter | solution.py:223
  94.5 184.5 %reduce-scatter.7.cloned.1.call-start = ((), (), s32[]{:S(2)}) async-start(), calls=%async_computation.7 | async-start | bytes 2293760 | tf_op jit(solution)/shard_map/reduce_scatter | solution.py:223
  114.9 165.2 %reduce-scatter.9.cloned.1.call-start = ((), (), s32[]{:S(2)}) async-start(), calls=%async_computation.8 | async-start | bytes 2293760 | tf_op jit(solution)/shard_map/reduce_scatter | solution.py:223
  135.5 145.8 %reduce-scatter.11.cloned.1.call-start = ((), (), s32[]{:S(2)}) async-start(), calls=%async_computation.9 | async-start | bytes 2293760 | tf_op jit(solution)/shard_map/reduce_scatter | solution.py:223
  198.9 69.1 %collective-permute-start = (bf16[224,4096]{1,0:T(8,128)(2,1)S(1)}, bf16[224,4096]{1,0:T(8,128)(2,1)}, u32[]{:S(2)}, u32[]{:S(2)}) collective-permute-start(bf16[224,4096]{1,0:T(8,128)(2,1)S(1)} %constant_dynamic-slice_fusion), channel_id=1, source_target_pairs={{0,1},{1,0},{2,3},{3,2},{4,5},{5,4},{6,7},{7,6},{8,9},{9,8},{10,11... | collective-permute-start | bytes 5505032 | tf_op jit(solution)/shard_map/ppermute | solution.py:232
  263.2 21.4 %all-to-all-start = ((f32[32,32,128]{2,1,0:T(8,128)}), f32[32,32,128]{2,1,0:T(8,128)S(1)}, u32[]{:S(2)}, u32[]{:S(2)}) async-start(f32[32,32,128]{2,1,0:T(8,128)} %bitcast.24), calls=%async_computation | async-start | bytes 1048576 | tf_op jit(solution)/shard_map/all_to_all | solution.py:245
Sparse Core Ops, SparseCore 0:
  9.5 60.9 all-gather.1
  94.6 42.2 reduce-scatter.4
  139.2 38.5 reduce-scatter.6
  180.0 38.5 reduce-scatter.8
  220.7 38.5 reduce-scatter.10
